TPU v7x, 32 devices: a whole 2x2x4 slice. The times are simulated.
32 devices in a mesh: groups: 2 (over y), tm: 16 (over z, x, core).
Axes of the slice: x: 2, y: 2, z: 4, core: 2. Of those that a mesh axis runs over, the one named last changes fastest.
Arguments:
- slot_frames: bfloat16 [256, 128, 1536], P(('groups', 'tm')), parts along dimension 0, may hold values from -6 to 6
- slot_live: int32 [256], P(('groups', 'tm')), parts along dimension 0, may hold values from 0 to 1, as said below
- utterance_start: int32 [4, 4096], P('groups', 'tm'), parts along dimension 0, may hold values from 0 to 4095, as said below
- in_projection: bfloat16 [1536, 2304], P('tm'), may hold values from -4 to 4, as said below
- out_projection: bfloat16 [768, 1536], P('tm'), may hold values from -0.21875 to 0.21875
- pointwise_in: bfloat16 [1536, 1536], P('tm'), may hold values from -0.15625 to 0.15625
- depthwise: float32 [31, 768], replicated, may hold values from -1 to 1
- pointwise_out: bfloat16 [768, 1536], P('tm'), may hold values from -0.21875 to 0.21875
- gain_attention: float32 [1536], replicated, may hold values from 0.25 to 1.75
- gain_convolution: float32 [1536], replicated, may hold values from 0.25 to 1.75
- gain_depth: float32 [768], replicated, may hold values from 0.25 to 1.75
Outputs:
- block_output: bfloat16 [4, 4096, 1536], P('groups', 'tm'), parts along dimension 0
There are 2 independent parts, one for each index of `groups`. A program takes and returns all parts, laid end to end along the dimension named above; an argument that names none is the same for every part. Nothing has to cross between parts.
Inputs may be any that keep to these rules, and one draw needn't show every extreme that they name: `slot_live`: with P(d) the number of live slots on time shards 0 to d - 1: 4 * (d - 2) <= P(d) <= 4 * (d + 2) for every d, both ends reached, and the whole group has exactly 4 live slots per time shard. A time shard has 0 to 8 live slots. utterance_start[s, t] <= t, never falls along t, and equals t where an utterance begins; it is 0 at t = 0. `in_projection`: entries of order 1 / sqrt(1536) or larger.
All inputs are finite; a program needn't handle non-finite values.
Results may differ from a plain program's by a relative error of at most 0.007.
Values may be sent and summed in bfloat16 or wider, within the bound.
No kernel may reach another device: no remote copies, remote signals or barrier semaphores. Data moves between devices by JAX's collectives and lax.ppermute only.
A program may use at most 128 MiB of HBM per device.

v0:
```python
import math

import jax
import jax.numpy as jnp
from jax import lax
from jax.experimental import pallas as pl
from jax.experimental.pallas import tpu as pltpu
from jax.sharding import PartitionSpec as P

H = 8
HD = 96
KERNEL = 31
CTX = 256
CHUNKS = 2
EDGE = 32
VMEM_LIMIT = 56 << 20

epsilon = 1e-05
bf16 = jnp.bfloat16
f32 = jnp.float32

ANY = pl.BlockSpec(memory_space=pl.ANY)
SMEM = pl.BlockSpec(memory_space=pltpu.SMEM)
VMEM = pl.BlockSpec(memory_space=pltpu.VMEM)


def layer_norm(values, gain_row):
    center = values - jnp.mean(values, axis=-1, keepdims=True)
    spread = jnp.mean(center * center, axis=-1, keepdims=True)
    return center * lax.rsqrt(spread + epsilon) * gain_row


def params():
    return pltpu.CompilerParams(vmem_limit_bytes=VMEM_LIMIT)


def after(value, *earlier):
    return lax.optimization_barrier((value, *earlier))[0]


def whole_weight(index):
    return [(index, side, lambda t: 0, lambda g, side=side: side) for side in (0, 1)]


def piece_copies():
    copies = []
    for flip, base in ((0, 0), (1, 5)):
        for side in (0, 1):
            copies.append((base, side, lambda t, f=flip: t ^ f, lambda g, s=side: s))
        for k in (1, 2, 3):
            plain = lambda t, k=k, f=flip: ((t - 4 * k) & 15) ^ f
            crossed = lambda t, k=k, f=flip: ((t - 4 * k) & 15) ^ (2 + f)
            copies.append((base + 1, k - 1, plain, lambda g: g))
            copies.append((base + 2, k - 1, crossed, lambda g: g))
            copies.append((base + 3, k - 1, plain, lambda g: 1 - g))
            copies.append((base + 4, k - 1, crossed, lambda g: 1 - g))
        next_door = lambda t, f=flip: t ^ (2 + f)
        copies.append((base + 1, 3, next_door, lambda g: g))
        copies.append((base + 3, 3, next_door, lambda g: 1 - g))
    return copies


def rest_pieces(parts, shift=0):
    pieces = []
    for part in range(parts):
        block = lambda t, part=part: part
        pieces.append((0, part, block, lambda g: g, lambda t: 0, shift))
        pieces.append((1, part, block, lambda g: 1 - g, lambda t: t & 1, 0))
        pieces.append((2, part, block, lambda g: 1 - g, lambda t: 1 - (t & 1), 0))
    return pieces


def load_weight(refs, pieces, segments, rows, place, target, sems):
    t, g = place
    started = []
    for array, lead, block, side, *quarter in pieces:
        for row, count, column, columns, row_offset, column_offset in segments:
            source = refs[array].at[lead]
            row = row + quarter[1] if quarter else row
            columns = source.shape[1] if columns is None else columns
            source = source.at[pl.ds(row, count), pl.ds(column, columns)]
            first = block(t)
            first = first * rows if isinstance(first, int) else pl.multiple_of(first * rows, rows)
            if quarter:
                column_offset = quarter[0](t)
                if not isinstance(column_offset, int):
                    column_offset = pl.multiple_of(column_offset * columns, 128)
            spot = target.at[side(g), pl.ds(first + row_offset, count), pl.ds(column_offset, columns)]
            copy = pltpu.make_async_copy(source, spot, sems.at[len(started)])
            copy.start()
            started.append(copy)
    return started


def prepare_kernel(place_ref, w_in, w_out, w_expand, w_last, half, half_rest, whole, sems):
    g = place_ref[1]
    width = half.shape[1]
    rows, columns = w_in.shape
    columns = columns // 2
    over = columns - width
    copies = []
    for target, side in ((half, g), (whole.at[0], 0), (whole.at[1], 1)):

        def lanes(base, size, side=side):
            return pl.ds(base if isinstance(side, int) else pl.multiple_of(base, 128), size)

        copies.append((w_in.at[:, lanes(side * columns, width)], target.at[pl.ds(0, rows)]))
        for part in (0, 1):
            source = w_in.at[pl.ds(part * rows // 2, rows // 2), lanes(side * columns + width, over)]
            copies.append((source, target.at[pl.ds(rows, rows // 2), pl.ds(part * over, over)]))
    row = 0
    for source in (w_out, w_expand, w_last):
        count = source.shape[0]
        copies.append((source.at[:, pl.ds(pl.multiple_of(g * width, 128), width)], half_rest.at[pl.ds(row, count)]))
        row += count
    started = [pltpu.make_async_copy(a, b, sems.at[i]) for i, (a, b) in enumerate(copies)]
    for copy in started:
        copy.start()
    for copy in started:
        copy.wait()


def hand_over_kernel(place_ref, frames, theirs, sem):
    part = theirs.shape[2]
    column = pl.multiple_of((1 - (place_ref[0] & 1)) * part, 128)
    copy = pltpu.make_async_copy(frames.at[:, :, pl.ds(column, part)], theirs, sem)
    copy.start()
    copy.wait()


def route_kernel(slots, chips, per_chunk, place_ref, live_ref, frames, theirs, *rest):
    chunks = rest[:CHUNKS]
    table_ref, leave_ref, sems = rest[CHUNKS:]
    t = place_ref[0]
    core = t & 1
    chip = t >> 1
    chip_slots = 2 * slots
    count = chip_slots // 2
    part = theirs.shape[2]
    mine = frames.at[:, :, pl.ds(pl.multiple_of(core * part, 128), part)]

    for j in range(count):
        table_ref[j] = 0
        leave_ref[j] = 0
    first = jnp.maximum(chip - 1, 0)
    total = lax.fori_loop(0, first * chip_slots, lambda f, s: s + live_ref[f], jnp.int32(0))

    for step in (-1, 0, 1):
        here = chip + step
        inside = (here >= 0) & (here < chips)
        start = jnp.clip(here, 0, chips - 1) * chip_slots
        if step == 0:
            offset = jnp.int32(0)
        else:
            offset = jnp.where(here == (chip ^ 1), chip_slots, chip_slots + count)

        def one(s, carry, step=step, here=here, inside=inside, start=start, offset=offset):
            counted, rank = carry
            live = jnp.where(inside, live_ref[start + s], 0)
            owner = counted // count
            leaving = jnp.where((live > 0) & (owner != here), 1, 0)

            @pl.when((live > 0) & (owner == chip))
            def _():
                table_ref[counted & (count - 1)] = (s if step == 0 else rank & (count - 1)) + offset

            if step == 0:

                @pl.when(leaving > 0)
                def _():
                    leave_ref[rank & (count - 1)] = s

            return counted + live, rank + leaving

        total, _ = lax.fori_loop(0, chip_slots, one, (total, jnp.int32(0)))
    for j in range(count):
        s = leave_ref[j]
        spot = chunks[j // per_chunk].at[j % per_chunk]
        own = (s // slots) == core

        @pl.when(own)
        def _():
            pltpu.make_async_copy(mine.at[s & (slots - 1)], spot, sems.at[j]).start()

        @pl.when(jnp.logical_not(own))
        def _():
            pltpu.make_async_copy(theirs.at[s & (slots - 1)], spot, sems.at[j]).start()

    for j in range(count):
        spot = chunks[j // per_chunk].at[j % per_chunk]
        pltpu.make_async_copy(mine.at[0], spot, sems.at[j]).wait()


def assemble_kernel(slots, per_chunk, place_ref, table_ref, frames, theirs, *rest):
    beside = rest[:CHUNKS]
    beyond = rest[CHUNKS : 2 * CHUNKS]
    keep, give, sems = rest[2 * CHUNKS :]
    core = place_ref[0] & 1
    part = theirs.shape[2]
    mine = frames.at[:, :, pl.ds(pl.multiple_of(core * part, 128), part)]
    count = slots
    blocks = count // 2
    for j in range(blocks):
        for side in (0, 1):
            target = (keep if side == 0 else give).at[j]
            sem = sems.at[side * blocks + j]
            code = table_ref[j + blocks * (core if side == 0 else 1 - core)]
            low = code & (slots - 1)
            local = code < 2 * slots
            own = (code // slots) == core

            @pl.when(local & own)
            def _():
                pltpu.make_async_copy(mine.at[low], target, sem).start()

            @pl.when(local & jnp.logical_not(own))
            def _():
                pltpu.make_async_copy(theirs.at[low], target, sem).start()

            for chunk in range(CHUNKS):
                for which, source in ((0, beside[chunk]), (1, beyond[chunk])):
                    low_end = 2 * slots + which * count + chunk * per_chunk

                    @pl.when((code >= low_end) & (code < low_end + per_chunk))
                    def _():
                        pltpu.make_async_copy(source.at[low & (per_chunk - 1)], target, sem).start()

    for j in range(blocks):
        pltpu.make_async_copy(mine.at[0], keep.at[j], sems.at[j]).wait()
        pltpu.make_async_copy(mine.at[0], give.at[j], sems.at[blocks + j]).wait()


def qkv_kernel(copies, segments, rows, place_ref, keep, other, gain, *rest):
    count = len(rest) - 6
    refs = rest[:count]
    stream, q, kv, weight, normed, sems = rest[count:]
    k, v = kv.at[0], kv.at[1]
    t, g = place_ref[0], place_ref[1]
    core = t & 1
    half = weight.shape[2]
    started = load_weight(refs, copies, segments, rows, (t, g), weight, sems)
    blocks, block_rows, part = keep.shape
    for b in range(blocks):
        a, o = keep[b], other[b]
        low = jnp.where(core == 0, a, o)
        high = jnp.where(core == 0, o, a)
        here = pl.ds(b * block_rows, block_rows)
        stream[here, pl.ds(0, part)] = low
        stream[here, pl.ds(part, part)] = high
        x = jnp.concatenate([low, high], axis=-1).astype(f32)
        normed[here] = layer_norm(x, gain[...]).astype(bf16)
    for copy in started:
        copy.wait()
    width = H * HD
    over = half - width
    tile = 256
    for b in range(blocks * block_rows // tile):
        here = pl.ds(b * tile, tile)
        x = normed[here]
        left = jnp.dot(x, weight[0], preferred_element_type=f32).astype(bf16)
        q[here] = left[:, :width]
        k[here, pl.ds(0, over)] = left[:, width:]
        right = jnp.dot(x, weight[1], preferred_element_type=f32).astype(bf16)
        k[here, pl.ds(over, width - over)] = right[:, : width - over]
        v[here] = right[:, width - over :]


def attention_kernel(frames, place_ref, q, kv, prior, starts, mixed, keys, values):
    k, v, prior_k, prior_v = kv.at[0], kv.at[1], prior.at[0], prior.at[1]
    t = place_ref[0]
    streams = q.shape[0] // frames
    tile = 128
    window = tile + CTX
    for s in range(streams):
        keys[pl.ds(2 * s * frames, frames)] = prior_k[pl.ds(s * frames, frames)]
        keys[pl.ds((2 * s + 1) * frames, frames)] = k[pl.ds(s * frames, frames)]
        values[pl.ds(2 * s * frames, frames)] = prior_v[pl.ds(s * frames, frames)]
        values[pl.ds((2 * s + 1) * frames, frames)] = v[pl.ds(s * frames, frames)]
    scale = 1.0 / math.sqrt(HD) / math.log(2.0)
    tiles = frames // tile

    def body(step, carry):
        s = step // tiles
        part = step % tiles
        here = pl.ds(pl.multiple_of(step * tile, tile), tile)
        there = pl.ds(pl.multiple_of(s * 2 * frames + part * tile, tile), window)
        row = lax.broadcasted_iota(jnp.int32, (tile, window), 0)
        col = lax.broadcasted_iota(jnp.int32, (tile, window), 1)
        begin = starts[here] - (t - 1) * frames - part * tile
        bias = jnp.where((col <= row + CTX) & (col >= row) & (col >= begin), 0.0, -1e30).astype(f32)
        for group in range(H // 4):
            outs = []
            for head in range(4):
                lane0 = head * HD
                first = lane0 // 128 * 128
                last = -(-(lane0 + HD) // 128) * 128
                lanes = pl.ds(group * 4 * HD + first, last - first)
                qs = q[here, lanes]
                lane = lax.broadcasted_iota(jnp.int32, qs.shape, 1) + first
                qs = jnp.where((lane >= lane0) & (lane < lane0 + HD), qs, jnp.zeros_like(qs))
                scores = lax.dot_general(
                    qs, keys[there, lanes], (((1,), (1,)), ((), ())), preferred_element_type=f32
                )
                scores = scores * scale + bias
                raised = jnp.exp2(scores - jnp.max(scores, axis=-1, keepdims=True))
                total = jnp.sum(raised, axis=-1, keepdims=True)
                out = jnp.dot(raised.astype(bf16), values[there, lanes], preferred_element_type=f32)
                outs.append(out * (1.0 / total))
            lane = lax.broadcasted_iota(jnp.int32, (tile, 128), 1)
            base = group * 4 * HD
            mixed[here, pl.ds(base, 128)] = jnp.where(lane < 96, outs[0], outs[1][:, :128]).astype(bf16)
            mixed[here, pl.ds(base + 128, 128)] = jnp.where(lane < 64, outs[1][:, 128:], outs[2][:, :128]).astype(
                bf16
            )
            mixed[here, pl.ds(base + 256, 128)] = jnp.where(lane < 32, outs[2][:, 128:], outs[3]).astype(bf16)
        return carry

    lax.fori_loop(0, streams * tiles, body, 0)


def gate_kernel(out_plan, in_plan, frames, place_ref, mixed, stream, gain, *rest):
    count = len(rest) - 7
    refs = rest[:count]
    middle, gated, edge, out_w, in_w, out_sems, in_sems = rest[count:]
    t, g = place_ref[0], place_ref[1]
    half = out_w.shape[2]
    out_started = load_weight(refs, *out_plan, (t, g), out_w, out_sems)
    in_started = load_weight(refs, *in_plan, (t, g), in_w, in_sems)
    for copy in out_started:
        copy.wait()
    tile = 256
    total = mixed.shape[0]
    for b in range(total // tile):
        here = pl.ds(b * tile, tile)
        x = mixed[here]
        for side in (0, 1):
            lanes = pl.ds(side * half, half)
            attended = jnp.dot(x, out_w[side], preferred_element_type=f32)
            middle[here, lanes] = (stream[here, lanes].astype(f32) + attended).astype(bf16)
    for copy in in_started:
        copy.wait()
    for b in range(total // tile):
        here = pl.ds(b * tile, tile)
        x = layer_norm(middle[here].astype(f32), gain[...]).astype(bf16)
        value = jnp.dot(x, in_w[0], preferred_element_type=f32)
        gate = jnp.dot(x, in_w[1], preferred_element_type=f32)
        gated[here] = (value * jax.nn.sigmoid(gate)).astype(bf16)
    for s in range(total // frames):
        edge[pl.ds(s * EDGE, EDGE)] = gated[pl.ds((s + 1) * frames - EDGE, EDGE)]


def conv_kernel(plan, frames, place_ref, gated, edge, middle, starts, taps, gain, *rest):
    count = len(rest) - 6
    refs = rest[:count]
    out, weight, padded, depth, elapsed, sems = rest[count:]
    t, g = place_ref[0], place_ref[1]
    half = weight.shape[2]
    started = load_weight(refs, *plan, (t, g), weight, sems)
    streams = gated.shape[0] // frames
    channels = gated.shape[1]
    lane_tiles = channels // 128
    block = 64
    blocks = frames // block
    for s in range(streams):
        for c in range(lane_tiles):
            lanes = pl.ds(c * 128, 128)
            padded[s * lane_tiles + c, pl.ds(0, EDGE)] = edge[pl.ds(s * EDGE, EDGE), lanes].astype(f32)
            padded[s * lane_tiles + c, pl.ds(EDGE, frames)] = gated[pl.ds(s * frames, frames), lanes].astype(f32)
    row = lax.broadcasted_iota(jnp.int32, (frames, 128), 0) + t * frames
    for s in range(streams):
        elapsed[pl.ds(s * frames, frames)] = row - jnp.broadcast_to(starts[pl.ds(s * frames, frames)], (frames, 128))

    for s in range(streams):

        def body(b, carry, s=s):
            r0 = pl.multiple_of(b * block, block)
            age = elapsed[pl.ds(s * frames + r0, block)]
            for c in range(lane_tiles):
                lanes = pl.ds(c * 128, 128)
                acc = jnp.zeros((block, 128), f32)
                for delay in range(KERNEL):
                    x = padded[s * lane_tiles + c, pl.ds(r0 + EDGE - delay, block)]
                    term = x * taps[pl.ds(KERNEL - 1 - delay, 1), lanes]
                    acc = acc + jnp.where(age >= delay, term, 0.0)
                depth[pl.ds(s * frames + r0, block), lanes] = acc
            return carry

        lax.fori_loop(0, blocks, body, 0)
    for copy in started:
        copy.wait()
    tile = 256
    for b in range(streams * frames // tile):
        here = pl.ds(b * tile, tile)
        n = layer_norm(depth[here], gain[...])
        swished = (n * jax.nn.sigmoid(n)).astype(bf16)
        for side in (0, 1):
            lanes = pl.ds(side * half, half)
            added = jnp.dot(swished, weight[side], preferred_element_type=f32)
            out[here, lanes] = (middle[here, lanes].astype(f32) + added).astype(bf16)


def dma_sems(count):
    return pltpu.SemaphoreType.DMA((count,))


def shards(
    slot_frames,
    slot_live,
    utterance_start,
    in_projection,
    out_projection,
    pointwise_in,
    depthwise,
    pointwise_out,
    gain_attention,
    gain_convolution,
    gain_depth,
):
    devices = lax.axis_size("tm")
    t = lax.axis_index("tm")
    g = lax.axis_index("groups")
    slots, block_rows, width = slot_frames.shape
    owner_blocks = slots // 2
    frames = 2 * block_rows
    streams = owner_blocks // 2
    rows = streams * frames
    part = width // 2
    core = t % 2
    in_half = in_projection.shape[1] // 2
    channels = H * HD
    conv_channels = pointwise_in.shape[1] // 2
    place = jnp.stack([t, g]).astype(jnp.int32)
    every = range(devices)
    across_core = [(i, i ^ 1) for i in every]
    across_x = [(i, i ^ 2) for i in every]
    onward = [(i, i - 4 if i & 2 else i + 4) for i in every]
    onward = [(i, j) for i, j in onward if 0 <= j < devices]
    next_door = [(i, i + 1) for i in range(devices - 1)]
    staged = devices == 16

    def like(shape, dtype=bf16):
        return jax.ShapeDtypeStruct(shape, dtype)

    def to_core(x):
        return lax.ppermute(x, "tm", across_core)

    def to_x(x):
        return lax.ppermute(x, "tm", across_x)

    def to_y(x):
        return lax.ppermute(x, "groups", [(0, 1), (1, 0)])

    def up(x, k):
        return lax.ppermute(x, "tm", [(i, (i + 4 * k) % devices) for i in every])

    def gathered_halves(w):
        full = lax.all_gather(w, "tm", axis=0, tiled=True)
        middle = full.shape[1] // 2
        return jnp.stack([full[:, :middle], full[:, middle:]])

    r_in, r_out, r_expand, r_last = (w.shape[0] for w in (in_projection, out_projection, pointwise_in, pointwise_out))
    r_rest = r_out + r_expand + r_last
    r_first = r_in + r_in // 2
    if staged:
        *half_packs, in_whole = pl.pallas_call(
            prepare_kernel,
            out_shape=[like((r_first, part)), like((r_rest, part)), like((2, r_first, part))],
            in_specs=[SMEM] + [ANY] * 4,
            out_specs=[VMEM] * 3,
            scratch_shapes=[dma_sems(18)],
            compiler_params=params(),
            name="prepare",
        )(place, in_projection, out_projection, pointwise_in, pointwise_out)
        half_in, half_rest = half_packs

    theirs = pl.pallas_call(
        hand_over_kernel,
        out_shape=like((slots, block_rows, part)),
        in_specs=[SMEM, ANY],
        out_specs=VMEM,
        scratch_shapes=[pltpu.SemaphoreType.DMA],
        compiler_params=params(),
        name="hand_over",
    )(place, slot_frames)
    theirs = to_core(theirs)

    live_all = lax.dynamic_update_slice(jnp.zeros((devices * slots,), jnp.int32), slot_live, (t * slots,))
    if staged:
        live_all = after(live_all, half_in)
    live_all = lax.psum(live_all, "tm")
    if staged:
        in_z = [up(after(half_in, live_all), k) for k in (1, 2, 3)]
        in_x = to_x(after(half_in, live_all))
        live_all = after(live_all, in_x)

    per_chunk = slots // CHUNKS
    *leaving, table = pl.pallas_call(
        lambda *r: route_kernel(slots, devices // 2, per_chunk, *r),
        out_shape=[like((per_chunk, block_rows, part))] * CHUNKS + [like((slots,), jnp.int32)],
        in_specs=[SMEM, SMEM, ANY, ANY],
        out_specs=[VMEM] * CHUNKS + [SMEM],
        scratch_shapes=[pltpu.SMEM((slots,), jnp.int32), dma_sems(slots)],
        compiler_params=params(),
        name="route",
    )(place, live_all, slot_frames, theirs)
    beside = [to_x(a) for a in leaving]
    beyond = [lax.ppermute(a, "tm", onward) for a in beside]

    if staged:
        in_column = jnp.stack(after(in_z, beside[0]))
        in_first = jnp.concatenate([in_column, in_x[None]])
        in_third = to_y(in_first)
        in_second = to_x(in_column)
        in_fourth = to_y(in_second)
        rest_mine = lax.all_gather(half_rest, "tm", axis=0, tiled=False)
        quarter = part // 2
        ready = after(rest_mine, *beyond)
        rest_over = []
        for low, high in ((0, r_out + r_expand), (r_out + r_expand, r_rest)):
            sent = lax.dynamic_slice(ready, (0, low, core * quarter), (devices, high - low, quarter))
            rest_over.append(to_y(sent))
        in_arrays = [in_whole, in_first, in_second, in_third, in_fourth]
        in_arrays += [to_core(a) for a in in_arrays]
        over = in_half - part
        half_rows = r_in // 2
        in_segments = [
            (0, r_in, 0, part, 0, 0),
            (r_in, half_rows, 0, over, 0, part),
            (r_in, half_rows, over, over, half_rows, part),
        ]
        in_plan = (piece_copies(), in_segments, r_in)
        pieces = rest_pieces(devices)
        plans = [
            (pieces, [(0, r_out, 0, None, 0, 0)], r_out),
            (pieces, [(r_out, r_expand, 0, None, 0, 0)], r_expand),
            (rest_pieces(devices, r_out + r_expand), [(0, r_last, 0, None, 0, 0)], r_last),
        ]
    else:
        in_arrays = [gathered_halves(in_projection)]
        rest_arrays = [gathered_halves(w) for w in (out_projection, pointwise_in, pointwise_out)]
        in_plan = (whole_weight(0), [(0, width, 0, in_half, 0, 0)], width)
        plans = [
            (whole_weight(i), [(0, count, 0, part, 0, 0)], count)
            for i, count in enumerate((channels, width, conv_channels))
        ]

    keep, give = pl.pallas_call(
        lambda *r: assemble_kernel(slots, per_chunk, *r),
        out_shape=[like((owner_blocks, block_rows, part))] * 2,
        in_specs=[SMEM, SMEM] + [ANY] * (2 + 2 * CHUNKS),
        out_specs=[VMEM] * 2,
        scratch_shapes=[dma_sems(slots)],
        compiler_params=params(),
        name="assemble",
    )(place, table, slot_frames, theirs, *beside, *beyond)
    other = to_core(give)

    stream, q, kv = pl.pallas_call(
        lambda *r: qkv_kernel(*in_plan, *r),
        out_shape=[like((rows, width)), like((rows, channels)), like((2, rows, channels))],
        in_specs=[SMEM, VMEM, VMEM, VMEM] + [ANY] * len(in_arrays),
        out_specs=[VMEM] * 3,
        scratch_shapes=[
            pltpu.VMEM((2, width, in_half), bf16),
            pltpu.VMEM((rows, width), bf16),
            dma_sems(len(in_plan[0]) * len(in_plan[1])),
        ],
        compiler_params=params(),
        name="qkv",
    )(place, keep, other, gain_attention[None], *in_arrays)

    prior = lax.ppermute(kv, "tm", next_door)
    starts = utterance_start.reshape(rows, 1)

    mixed = pl.pallas_call(
        lambda *r: attention_kernel(frames, *r),
        out_shape=like((rows, channels)),
        in_specs=[SMEM] + [VMEM] * 4,
        out_specs=VMEM,
        scratch_shapes=[pltpu.VMEM((2 * rows, channels), bf16)] * 2,
        compiler_params=params(),
        name="attention",
    )(place, q, kv, prior, starts)

    if staged:
        mid_arrays = [rest_mine, rest_over[0], to_core(after(rest_over[0], mixed))]
    else:
        mid_arrays = last_arrays = rest_arrays

    middle, gated, edge = pl.pallas_call(
        lambda *r: gate_kernel(plans[0], plans[1], frames, *r),
        out_shape=[like((rows, width)), like((rows, conv_channels)), like((streams * EDGE, conv_channels))],
        in_specs=[SMEM, VMEM, VMEM, VMEM] + [ANY] * len(mid_arrays),
        out_specs=[VMEM] * 3,
        scratch_shapes=[
            pltpu.VMEM((2, channels, part), bf16),
            pltpu.VMEM((2, width, part), bf16),
            dma_sems(len(plans[0][0])),
            dma_sems(len(plans[1][0])),
        ],
        compiler_params=params(),
        name="gate",
    )(place, mixed, stream, gain_convolution[None], *mid_arrays)
    edge = lax.ppermute(edge, "tm", next_door)
    if staged:
        last_arrays = [rest_mine, rest_over[1], to_core(after(rest_over[1], gated))]

    lane_tiles = conv_channels // 128
    out = pl.pallas_call(
        lambda *r: conv_kernel(plans[2], frames, *r),
        out_shape=like((rows, width)),
        in_specs=[SMEM] + [VMEM] * 6 + [ANY] * len(last_arrays),
        out_specs=VMEM,
        scratch_shapes=[
            pltpu.VMEM((2, conv_channels, part), bf16),
            pltpu.VMEM((streams * lane_tiles, EDGE + frames, 128), f32),
            pltpu.VMEM((rows, conv_channels), f32),
            pltpu.VMEM((rows, 128), jnp.int32),
            dma_sems(len(plans[2][0])),
        ],
        compiler_params=params(),
        name="conv",
    )(place, gated, edge, middle, starts, depthwise, gain_depth[None], *last_arrays)
    return out.reshape(streams, frames, width)


def solution(mesh):
    in_specs = (
        P(("groups", "tm"), None, None),
        P(("groups", "tm")),
        P("groups", "tm"),
        P("tm", None),
        P("tm", None),
        P("tm", None),
        P(),
        P("tm", None),
        P(),
        P(),
        P(),
    )
    out_specs = P("groups", "tm", None)
    return jax.shard_map(shards, mesh=mesh, in_specs=in_specs, out_specs=out_specs, check_vma=False)
```

profile of v0, /device:TPU:8, one launch (start us, length us, event | category | flops | bytes accessed | tf_op | source)
XLA Modules:
  0.0 214.0 jit_solution(13496097215390032545)
XLA Ops:
  7.2 3.0 %prepare.1 = (bf16[144,768]{1,0:T(8,128)(2,1)}, bf16[192,768]{1,0:T(8,128)(2,1)}, bf16[2,144,768]{2,1,0:T(8,128)(2,1)}) custom-call(s32[2]{0:T(128)} %pad_add_fusion.place_ref.r_0_, bf16[96,2304]{1,0:T(8,128)(2,1)} %w_in.1, bf16[48,1536]{1,0:T(8,128)(2,1)} %w_out.1, bf16[96,1536]{1,0:T(8,128)(2,1)} %w_expand.1, bf16[48,1536]{1,0:T(8,128)(2,1)} %w_last.1), custom_call_target="tpu_custom_call" | custom-call | tf_op jit(solution)/shard_map/prepare/pallas_call | solution.py:465
  10.3 3.4 %hand_over.1 = bf16[8,128,768]{2,1,0:T(8,128)(2,1)} custom-call(s32[2]{0:T(128)} %pad_add_fusion.place_ref.r_0_, bf16[8,128,1536]{2,1,0:T(8,128)(2,1)} %r_2_.3), custom_call_target="tpu_custom_call" | custom-call | tf_op jit(solution)/shard_map/hand_over/pallas_call | solution.py:476
  14.0 13.1 %psum.7.r_1_ = s32[128]{0:T(128)} all-reduce(s32[128]{0:T(128)S(1)} %dynamic_update_slice.3), channel_id=1, replica_groups=mesh['groups'=2,'tm'=16] {'tm'}, use_global_device_ids=true, to_apply=%region_0.1 | all-reduce | flops 128 | bytes 1024 | tf_op jit(solution)/shard_map/psum | solution.py:490
  27.6 5.4 %collective-permute-done = bf16[144,768]{1,0:T(8,128)(2,1)S(1)} collective-permute-done((bf16[144,768]{1,0:T(8,128)(2,1)S(1)}, bf16[144,768]{1,0:T(8,128)(2,1)S(1)}, u32[]{:S(2)}, u32[]{:S(2)}) %collective-permute-start) | collective-permute-done | bytes 221216 | tf_op jit(solution)/shard_map/ppermute | solution.py:448
  34.2 4.8 %route.1 = (bf16[4,128,768]{2,1,0:T(8,128)(2,1)}, bf16[4,128,768]{2,1,0:T(8,128)(2,1)}, s32[8]{0:T(128)}) custom-call(s32[2]{0:T(128)} %pad_add_fusion.place_ref.r_0_, s32[128]{0:T(128)} %psum.7.r_1_, bf16[8,128,1536]{2,1,0:T(8,128)(2,1)} %r_2_.3, bf16[8,128,768]{2,1,0:T(8,128)(2,1)} %copy-done), custom_call_target="tpu_custom_call" | custom-call | tf_op jit(solution)/shard_map/route/pallas_call | solution.py:497
  39.0 2.0 collective-permute-start.3
  41.4 2.9 %collective-permute-start.8 = (bf16[144,768]{1,0:T(8,128)(2,1)S(1)}, bf16[144,768]{1,0:T(8,128)(2,1)S(1)}, u32[]{:S(2)}, u32[]{:S(2)}) collective-permute-start(bf16[144,768]{1,0:T(8,128)(2,1)S(1)} %copy-done.17), channel_id=1, source_target_pairs={{0,8},{1,9},{2,10},{3,11},{4,12},{5,13},{6,14},{7,15},{8,0},{9,1},... | collective-permute-start | bytes 663560 | tf_op jit(solution)/shard_map/ppermute | solution.py:454
  44.3 19.5 %collective-permute-done.7 = bf16[144,768]{1,0:T(8,128)(2,1)S(1)} collective-permute-done((bf16[144,768]{1,0:T(8,128)(2,1)S(1)}, bf16[144,768]{1,0:T(8,128)(2,1)S(1)}, u32[]{:S(2)}, u32[]{:S(2)}) %collective-permute-start.7) | collective-permute-done | bytes 221216 | tf_op jit(solution)/shard_map/ppermute | solution.py:454
  63.8 11.8 %collective-permute-done.8 = bf16[144,768]{1,0:T(8,128)(2,1)S(1)} collective-permute-done((bf16[144,768]{1,0:T(8,128)(2,1)S(1)}, bf16[144,768]{1,0:T(8,128)(2,1)S(1)}, u32[]{:S(2)}, u32[]{:S(2)}) %collective-permute-start.8) | collective-permute-done | bytes 221216 | tf_op jit(solution)/shard_map/ppermute | solution.py:454
  75.6 3.4 %collective-permute-done.9 = bf16[144,768]{1,0:T(8,128)(2,1)S(1)} collective-permute-done((bf16[144,768]{1,0:T(8,128)(2,1)S(1)}, bf16[144,768]{1,0:T(8,128)(2,1)S(1)}, u32[]{:S(2)}, u32[]{:S(2)}) %collective-permute-start.9) | collective-permute-done | bytes 221216 | tf_op jit(solution)/shard_map/ppermute | solution.py:454
  83.6 4.4 %collective-permute-done.3.r_5_ = bf16[4,128,768]{2,1,0:T(8,128)(2,1)S(1)} collective-permute-done((bf16[4,128,768]{2,1,0:T(8,128)(2,1)}, bf16[4,128,768]{2,1,0:T(8,128)(2,1)S(1)}, u32[]{:S(2)}, u32[]{:S(2)}) %collective-permute-start.3) | collective-permute-done | bytes 786464 | tf_op jit(solution)/shard_map/ppermute | solution.py:448
  87.9 2.9 %collective-permute-start.5 = (bf16[4,128,768]{2,1,0:T(8,128)(2,1)S(1)}, bf16[4,128,768]{2,1,0:T(8,128)(2,1)S(1)}, u32[]{:S(2)}, u32[]{:S(2)}) collective-permute-start(bf16[4,128,768]{2,1,0:T(8,128)(2,1)S(1)} %collective-permute-done.3.r_5_), channel_id=1, source_target_pairs={{0,4},{1,5},{4,8},{5,9},{6,2},{7,3},{8,12},{9,13},{10,6},{11,7},{1... | collective-permute-start | bytes 2359304 | tf_op jit(solution)/shard_map/ppermute | solution.py:507
  90.8 8.5 %collective-permute-done.10.r_6_ = bf16[3,144,768]{2,1,0:T(8,128)(2,1)} collective-permute-done((bf16[3,144,768]{2,1,0:T(8,128)(2,1)S(1)}, bf16[3,144,768]{2,1,0:T(8,128)(2,1)}, u32[]{:S(2)}, u32[]{:S(2)}) %collective-permute-start.10) | collective-permute-done | bytes 663584 | tf_op jit(solution)/shard_map/ppermute | solution.py:448
  102.1 2.3 %collective-permute-done.11.r_7_ = bf16[4,144,768]{2,1,0:T(8,128)(2,1)S(1)} collective-permute-done((bf16[4,144,768]{2,1,0:T(8,128)(2,1)S(1)}, bf16[4,144,768]{2,1,0:T(8,128)(2,1)S(1)}, u32[]{:S(2)}, u32[]{:S(2)}) %collective-permute-start.11) | collective-permute-done | bytes 884768 | tf_op jit(solution)/shard_map/ppermute | solution.py:451
  104.4 12.3 %collective-permute-done.5.r_7_ = bf16[4,128,768]{2,1,0:T(8,128)(2,1)S(1)} collective-permute-done((bf16[4,128,768]{2,1,0:T(8,128)(2,1)S(1)}, bf16[4,128,768]{2,1,0:T(8,128)(2,1)S(1)}, u32[]{:S(2)}, u32[]{:S(2)}) %collective-permute-start.5) | collective-permute-done | bytes 786464 | tf_op jit(solution)/shard_map/ppermute | solution.py:507
  117.6 3.4 %assemble.1 = (bf16[4,128,768]{2,1,0:T(8,128)(2,1)}, bf16[4,128,768]{2,1,0:T(8,128)(2,1)}) custom-call(s32[2]{0:T(128)} %pad_add_fusion.place_ref.r_0_, s32[8]{0:T(128)} %get-tuple-element.32.r_1_, bf16[8,128,1536]{2,1,0:T(8,128)(2,1)} %r_2_.3, bf16[8,128,768]{2,1,0:T(8,128)(2,1)} %copy-done, bf16[4,128,768]{2,1,0:T(8,128)(2,1)} %copy-done.4, ...), custom_call_target="tpu_custom_call" | custom-call | tf_op jit(solution)/shard_map/assemble/pallas_call | solution.py:547
  126.0 10.9 %qkv.1 = (bf16[512,1536]{1,0:T(8,128)(2,1)}, bf16[512,768]{1,0:T(8,128)(2,1)}, bf16[2,512,768]{2,1,0:T(8,128)(2,1)}) custom-call(s32[2]{0:T(128)} %pad_add_fusion.place_ref.r_0_, bf16[4,128,768]{2,1,0:T(8,128)(2,1)} %get-tuple-element.35.r_1_, bf16[4,128,768]{2,1,0:T(8,128)(2,1)} %collective-permute-done.6.r_2_, f32[1,1536]{1,0:T(1,128)} %broadcast_in_dim.16.r_3_, ...), custom_call_target="tpu_custom_call" | custom-call | tf_op jit(solution)/shard_map/qkv/pallas_call | solution.py:558
  136.8 2.3 %collective-permute-start.18 = (bf16[2,512,768]{2,1,0:T(8,128)(2,1)}, bf16[2,512,768]{2,1,0:T(8,128)(2,1)}, u32[]{:S(2)}, u32[]{:S(2)}) collective-permute-start(bf16[2,512,768]{2,1,0:T(8,128)(2,1)} %get-tuple-element.42.r_2_), channel_id=1, source_target_pairs={{0,1},{1,2},{2,3},{3,4},{4,5},{5,6},{6,7},{7,8},{8,9},{9,10},{10,1... | collective-permute-start | bytes 4718600 | tf_op jit(solution)/shard_map/ppermute | solution.py:572
  140.0 19.8 %collective-permute-done.18.r_3_ = bf16[2,512,768]{2,1,0:T(8,128)(2,1)} collective-permute-done((bf16[2,512,768]{2,1,0:T(8,128)(2,1)}, bf16[2,512,768]{2,1,0:T(8,128)(2,1)}, u32[]{:S(2)}, u32[]{:S(2)}) %collective-permute-start.18) | collective-permute-done | bytes 1572896 | tf_op jit(solution)/shard_map/ppermute | solution.py:572
  159.8 11.0 %attention.1.r_1_ = bf16[512,768]{1,0:T(8,128)(2,1)} custom-call(s32[2]{0:T(128)} %pad_add_fusion.place_ref.r_0_, bf16[512,768]{1,0:T(8,128)(2,1)} %get-tuple-element.41.r_1_, bf16[2,512,768]{2,1,0:T(8,128)(2,1)} %get-tuple-element.42.r_2_, bf16[2,512,768]{2,1,0:T(8,128)(2,1)} %collective-permute-done.18.r_3_, s32[512,1]{1,0:T(8,128)} %bitcast.16), custom_call_target="tpu_custom_call" | custom-call | tf_op jit(solution)/shard_map/attention/pallas_call | solution.py:575
  176.0 11.0 %gate.1 = (bf16[512,1536]{1,0:T(8,128)(2,1)}, bf16[512,768]{1,0:T(8,128)(2,1)}, bf16[64,768]{1,0:T(8,128)(2,1)}) custom-call(s32[2]{0:T(128)} %pad_add_fusion.place_ref.r_0_, bf16[512,768]{1,0:T(8,128)(2,1)} %attention.1.r_1_, bf16[512,1536]{1,0:T(8,128)(2,1)} %get-tuple-element.43.r_2_, f32[1,1536]{1,0:T(1,128)} %broadcast_in_dim.18.r_3_, ...), custom_call_target="tpu_custom_call" | custom-call | tf_op jit(solution)/shard_map/gate/pallas_call | solution.py:590
  187.8 2.4 %collective-permute-start.21 = (bf16[64,768]{1,0:T(8,128)(2,1)}, bf16[64,768]{1,0:T(8,128)(2,1)S(1)}, u32[]{:S(2)}, u32[]{:S(2)}) collective-permute-start(bf16[64,768]{1,0:T(8,128)(2,1)} %get-tuple-element.48), channel_id=1, source_target_pairs={{0,1},{1,2},{2,3},{3,4},{4,5},{5,6},{6,7},{7,8},{8,9},{9,10},{10,1... | collective-permute-start | bytes 294920 | tf_op jit(solution)/shard_map/ppermute | solution.py:604
  190.8 4.0 %collective-permute-done.21.r_2_ = bf16[64,768]{1,0:T(8,128)(2,1)S(1)} collective-permute-done((bf16[64,768]{1,0:T(8,128)(2,1)}, bf16[64,768]{1,0:T(8,128)(2,1)S(1)}, u32[]{:S(2)}, u32[]{:S(2)}) %collective-permute-start.21) | collective-permute-done | bytes 98336 | tf_op jit(solution)/shard_map/ppermute | solution.py:604
  195.7 11.5 %conv.1 = bf16[512,1536]{1,0:T(8,128)(2,1)} custom-call(s32[2]{0:T(128)} %pad_add_fusion.place_ref.r_0_, bf16[512,768]{1,0:T(8,128)(2,1)} %get-tuple-element.47.r_1_, bf16[64,768]{1,0:T(8,128)(2,1)} %copy-done.12, bf16[512,1536]{1,0:T(8,128)(2,1)} %get-tuple-element.49.r_3_, s32[512,1]{1,0:T(8,128)} %bitcast.17, f32[31,768]{1,0:T(8,128)} %r_5_.1, ...), custom_call_target="tpu_custom_call" | custom-call | tf_op jit(solution)/shard_map/conv/pallas_call | solution.py:609
  (86 shorter events, 24.5 us)
Async XLA Ops:
  6.5 115.9 %all-gather.3.cloned.1.call-start = ((), (), s32[]{:S(2)}) async-start(), calls=%async_computation | async-start | bytes 5013504 | tf_op jit(solution)/shard_map/all_gather | solution.py:515
  13.7 19.4 %collective-permute-start.1 = (bf16[8,128,768]{2,1,0:T(8,128)(2,1)}, bf16[8,128,768]{2,1,0:T(8,128)(2,1)S(1)}, u32[]{:S(2)}, u32[]{:S(2)}) collective-permute-start(bf16[8,128,768]{2,1,0:T(8,128)(2,1)} %hand_over.1), channel_id=1, source_target_pairs={{0,1},{1,0},{2,3},{3,2},{4,5},{5,4},{6,7},{7,6},{8,9},{9,8},{10,11... | collective-permute-start | bytes 4718600 | tf_op jit(solution)/shard_map/ppermute | solution.py:445
  27.1 5.9 %collective-permute-start = (bf16[144,768]{1,0:T(8,128)(2,1)S(1)}, bf16[144,768]{1,0:T(8,128)(2,1)S(1)}, u32[]{:S(2)}, u32[]{:S(2)}) collective-permute-start(bf16[144,768]{1,0:T(8,128)(2,1)S(1)} %copy-done.17), channel_id=1, source_target_pairs={{0,2},{1,3},{2,0},{3,1},{4,6},{5,7},{6,4},{7,5},{8,10},{9,11},{10,... | collective-permute-start | bytes 663560 | tf_op jit(solution)/shard_map/ppermute | solution.py:448
  39.0 40.0 %collective-permute-start.2 = (bf16[4,128,768]{2,1,0:T(8,128)(2,1)}, bf16[4,128,768]{2,1,0:T(8,128)(2,1)S(1)}, u32[]{:S(2)}, u32[]{:S(2)}) collective-permute-start(bf16[4,128,768]{2,1,0:T(8,128)(2,1)} %get-tuple-element.33), channel_id=1, source_target_pairs={{0,2},{1,3},{2,0},{3,1},{4,6},{5,7},{6,4},{7,5},{8,10},{9,11},{10,... | collective-permute-start | bytes 2359304 | tf_op jit(solution)/shard_map/ppermute | solution.py:448
  39.0 48.9 %collective-permute-start.3 = (bf16[4,128,768]{2,1,0:T(8,128)(2,1)}, bf16[4,128,768]{2,1,0:T(8,128)(2,1)S(1)}, u32[]{:S(2)}, u32[]{:S(2)}) collective-permute-start(bf16[4,128,768]{2,1,0:T(8,128)(2,1)} %get-tuple-element.34), channel_id=1, source_target_pairs={{0,2},{1,3},{2,0},{3,1},{4,6},{5,7},{6,4},{7,5},{8,10},{9,11},{10,... | collective-permute-start | bytes 2359304 | tf_op jit(solution)/shard_map/ppermute | solution.py:448
  41.0 22.7 %collective-permute-start.7 = (bf16[144,768]{1,0:T(8,128)(2,1)S(1)}, bf16[144,768]{1,0:T(8,128)(2,1)S(1)}, u32[]{:S(2)}, u32[]{:S(2)}) collective-permute-start(bf16[144,768]{1,0:T(8,128)(2,1)S(1)} %copy-done.17), channel_id=1, source_target_pairs={{0,4},{1,5},{2,6},{3,7},{4,8},{5,9},{6,10},{7,11},{8,12},{9,13},{1... | collective-permute-start | bytes 663560 | tf_op jit(solution)/shard_map/ppermute | solution.py:454
  41.4 34.2 %collective-permute-start.8 = (bf16[144,768]{1,0:T(8,128)(2,1)S(1)}, bf16[144,768]{1,0:T(8,128)(2,1)S(1)}, u32[]{:S(2)}, u32[]{:S(2)}) collective-permute-start(bf16[144,768]{1,0:T(8,128)(2,1)S(1)} %copy-done.17), channel_id=1, source_target_pairs={{0,8},{1,9},{2,10},{3,11},{4,12},{5,13},{6,14},{7,15},{8,0},{9,1},... | collective-permute-start | bytes 663560 | tf_op jit(solution)/shard_map/ppermute | solution.py:454
  44.3 34.7 %collective-permute-start.9 = (bf16[144,768]{1,0:T(8,128)(2,1)S(1)}, bf16[144,768]{1,0:T(8,128)(2,1)S(1)}, u32[]{:S(2)}, u32[]{:S(2)}) collective-permute-start(bf16[144,768]{1,0:T(8,128)(2,1)S(1)} %copy-done.17), channel_id=1, source_target_pairs={{0,12},{1,13},{2,14},{3,15},{4,0},{5,1},{6,2},{7,3},{8,4},{9,5},{1... | collective-permute-start | bytes 663560 | tf_op jit(solution)/shard_map/ppermute | solution.py:454
  79.1 20.2 %collective-permute-start.10 = (bf16[3,144,768]{2,1,0:T(8,128)(2,1)S(1)}, bf16[3,144,768]{2,1,0:T(8,128)(2,1)}, u32[]{:S(2)}, u32[]{:S(2)}) collective-permute-start(bf16[3,144,768]{2,1,0:T(8,128)(2,1)S(1)} %pad_maximum_fusion.1), channel_id=1, source_target_pairs={{0,2},{1,3},{2,0},{3,1},{4,6},{5,7},{6,4},{7,5},{8,10},{9,11},{10,... | collective-permute-start | bytes 1990664 | tf_op jit(solution)/shard_map/ppermute | solution.py:448
  79.7 22.4 %collective-permute-start.4 = (bf16[4,128,768]{2,1,0:T(8,128)(2,1)S(1)}, bf16[4,128,768]{2,1,0:T(8,128)(2,1)S(1)}, u32[]{:S(2)}, u32[]{:S(2)}) collective-permute-start(bf16[4,128,768]{2,1,0:T(8,128)(2,1)S(1)} %collective-permute-done.2.r_4_), channel_id=1, source_target_pairs={{0,4},{1,5},{4,8},{5,9},{6,2},{7,3},{8,12},{9,13},{10,6},{11,7},{1... | collective-permute-start | bytes 2359304 | tf_op jit(solution)/shard_map/ppermute | solution.py:507
  81.7 22.6 %collective-permute-start.11 = (bf16[4,144,768]{2,1,0:T(8,128)(2,1)S(1)}, bf16[4,144,768]{2,1,0:T(8,128)(2,1)S(1)}, u32[]{:S(2)}, u32[]{:S(2)}) collective-permute-start(bf16[4,144,768]{2,1,0:T(8,128)(2,1)S(1)} %pad_maximum_fusion.r_5_), channel_id=1, source_target_pairs={{0,16},{16,0},{1,17},{17,1},{2,18},{18,2},{3,19},{19,3},{4,20},{20... | collective-permute-start | bytes 2654216 | tf_op jit(solution)/shard_map/ppermute | solution.py:451
  87.9 28.7 %collective-permute-start.5 = (bf16[4,128,768]{2,1,0:T(8,128)(2,1)S(1)}, bf16[4,128,768]{2,1,0:T(8,128)(2,1)S(1)}, u32[]{:S(2)}, u32[]{:S(2)}) collective-permute-start(bf16[4,128,768]{2,1,0:T(8,128)(2,1)S(1)} %collective-permute-done.3.r_5_), channel_id=1, source_target_pairs={{0,4},{1,5},{4,8},{5,9},{6,2},{7,3},{8,12},{9,13},{10,6},{11,7},{1... | collective-permute-start | bytes 2359304 | tf_op jit(solution)/shard_map/ppermute | solution.py:507
  99.3 23.2 %collective-permute-start.12 = (bf16[3,144,768]{2,1,0:T(8,128)(2,1)}, bf16[3,144,768]{2,1,0:T(8,128)(2,1)}, u32[]{:S(2)}, u32[]{:S(2)}) collective-permute-start(bf16[3,144,768]{2,1,0:T(8,128)(2,1)} %collective-permute-done.10.r_6_), channel_id=1, source_target_pairs={{0,16},{16,0},{1,17},{17,1},{2,18},{18,2},{3,19},{19,3},{4,20},{20... | collective-permute-start | bytes 1990664 | tf_op jit(solution)/shard_map/ppermute | solution.py:451
  101.0 20.1 %collective-permute-start.13 = (bf16[2,144,768]{2,1,0:T(8,128)(2,1)S(1)}, bf16[2,144,768]{2,1,0:T(8,128)(2,1)S(1)}, u32[]{:S(2)}, u32[]{:S(2)}) collective-permute-start(bf16[2,144,768]{2,1,0:T(8,128)(2,1)S(1)} %copy-done.10), channel_id=1, source_target_pairs={{0,1},{1,0},{2,3},{3,2},{4,5},{5,4},{6,7},{7,6},{8,9},{9,8},{10,11... | collective-permute-start | bytes 1327112 | tf_op jit(solution)/shard_map/ppermute | solution.py:445
  102.1 22.1 %collective-permute-start.14 = (bf16[4,144,768]{2,1,0:T(8,128)(2,1)S(1)}, bf16[4,144,768]{2,1,0:T(8,128)(2,1)}, u32[]{:S(2)}, u32[]{:S(2)}) collective-permute-start(bf16[4,144,768]{2,1,0:T(8,128)(2,1)S(1)} %pad_maximum_fusion.r_5_), channel_id=1, source_target_pairs={{0,1},{1,0},{2,3},{3,2},{4,5},{5,4},{6,7},{7,6},{8,9},{9,8},{10,11... | collective-permute-start | bytes 2654216 | tf_op jit(solution)/shard_map/ppermute | solution.py:445
  104.4 21.6 %collective-permute-start.16 = (bf16[4,144,768]{2,1,0:T(8,128)(2,1)S(1)}, bf16[4,144,768]{2,1,0:T(8,128)(2,1)}, u32[]{:S(2)}, u32[]{:S(2)}) collective-permute-start(bf16[4,144,768]{2,1,0:T(8,128)(2,1)S(1)} %collective-permute-done.11.r_7_), channel_id=1, source_target_pairs={{0,1},{1,0},{2,3},{3,2},{4,5},{5,4},{6,7},{7,6},{8,9},{9,8},{10,11... | collective-permute-start | bytes 2654216 | tf_op jit(solution)/shard_map/ppermute | solution.py:445
  121.1 4.9 %collective-permute-start.6 = (bf16[4,128,768]{2,1,0:T(8,128)(2,1)}, bf16[4,128,768]{2,1,0:T(8,128)(2,1)}, u32[]{:S(2)}, u32[]{:S(2)}) collective-permute-start(bf16[4,128,768]{2,1,0:T(8,128)(2,1)} %get-tuple-element.36), channel_id=1, source_target_pairs={{0,1},{1,0},{2,3},{3,2},{4,5},{5,4},{6,7},{7,6},{8,9},{9,8},{10,11... | collective-permute-start | bytes 2359304 | tf_op jit(solution)/shard_map/ppermute | solution.py:445
  121.9 4.0 %collective-permute-start.15 = (bf16[3,144,768]{2,1,0:T(8,128)(2,1)}, bf16[3,144,768]{2,1,0:T(8,128)(2,1)}, u32[]{:S(2)}, u32[]{:S(2)}) collective-permute-start(bf16[3,144,768]{2,1,0:T(8,128)(2,1)} %collective-permute-done.10.r_6_), channel_id=1, source_target_pairs={{0,1},{1,0},{2,3},{3,2},{4,5},{5,4},{6,7},{7,6},{8,9},{9,8},{10,11... | collective-permute-start | bytes 1990664 | tf_op jit(solution)/shard_map/ppermute | solution.py:445
  124.2 46.7 %collective-permute-start.19 = (bf16[16,144,384]{2,1,0:T(8,128)(2,1)S(1)}, bf16[16,144,384]{2,1,0:T(8,128)(2,1)}, u32[]{:S(2)}, u32[]{:S(2)}) collective-permute-start(bf16[16,144,384]{2,1,0:T(8,128)(2,1)S(1)} %constant_dynamic-slice_fusion.1), channel_id=1, source_target_pairs={{0,16},{16,0},{1,17},{17,1},{2,18},{18,2},{3,19},{19,3},{4,20},{20... | collective-permute-start | bytes 5308424 | tf_op jit(solution)/shard_map/ppermute | solution.py:451
  136.8 23.0 %collective-permute-start.18 = (bf16[2,512,768]{2,1,0:T(8,128)(2,1)}, bf16[2,512,768]{2,1,0:T(8,128)(2,1)}, u32[]{:S(2)}, u32[]{:S(2)}) collective-permute-start(bf16[2,512,768]{2,1,0:T(8,128)(2,1)} %get-tuple-element.42.r_2_), channel_id=1, source_target_pairs={{0,1},{1,2},{2,3},{3,4},{4,5},{5,6},{6,7},{7,8},{8,9},{9,10},{10,1... | collective-permute-start | bytes 4718600 | tf_op jit(solution)/shard_map/ppermute | solution.py:572
  170.8 3.9 %collective-permute-start.20 = (bf16[16,144,384]{2,1,0:T(8,128)(2,1)}, bf16[16,144,384]{2,1,0:T(8,128)(2,1)S(1)}, u32[]{:S(2)}, u32[]{:S(2)}) collective-permute-start(bf16[16,144,384]{2,1,0:T(8,128)(2,1)} %collective-permute-done.19.r_5_), channel_id=1, source_target_pairs={{0,1},{1,0},{2,3},{3,2},{4,5},{5,4},{6,7},{7,6},{8,9},{9,8},{10,11... | collective-permute-start | bytes 5308424 | tf_op jit(solution)/shard_map/ppermute | solution.py:445
  172.0 15.8 %collective-permute-start.22 = (bf16[16,48,384]{2,1,0:T(8,128)(2,1)S(1)}, bf16[16,48,384]{2,1,0:T(8,128)(2,1)S(1)}, u32[]{:S(2)}, u32[]{:S(2)}) collective-permute-start(bf16[16,48,384]{2,1,0:T(8,128)(2,1)S(1)} %constant_dynamic-slice_fusion), channel_id=1, source_target_pairs={{0,16},{16,0},{1,17},{17,1},{2,18},{18,2},{3,19},{19,3},{4,20},{20... | collective-permute-start | bytes 1769480 | tf_op jit(solution)/shard_map/ppermute | solution.py:451
  187.8 7.0 %collective-permute-start.23 = (bf16[16,48,384]{2,1,0:T(8,128)(2,1)S(1)}, bf16[16,48,384]{2,1,0:T(8,128)(2,1)S(1)}, u32[]{:S(2)}, u32[]{:S(2)}) collective-permute-start(bf16[16,48,384]{2,1,0:T(8,128)(2,1)S(1)} %collective-permute-done.22.r_8_), channel_id=1, source_target_pairs={{0,1},{1,0},{2,3},{3,2},{4,5},{5,4},{6,7},{7,6},{8,9},{9,8},{10,11... | collective-permute-start | bytes 1769480 | tf_op jit(solution)/shard_map/ppermute | solution.py:445
  187.8 7.0 %collective-permute-start.21 = (bf16[64,768]{1,0:T(8,128)(2,1)}, bf16[64,768]{1,0:T(8,128)(2,1)S(1)}, u32[]{:S(2)}, u32[]{:S(2)}) collective-permute-start(bf16[64,768]{1,0:T(8,128)(2,1)} %get-tuple-element.48), channel_id=1, source_target_pairs={{0,1},{1,2},{2,3},{3,4},{4,5},{5,6},{6,7},{7,8},{8,9},{9,10},{10,1... | collective-permute-start | bytes 294920 | tf_op jit(solution)/shard_map/ppermute | solution.py:604
  (20 other events, 279.1 us)
Sparse Core Ops, SparseCore 0:
  10.4 67.3 all-gather.2
where the time goes:
time: 215 us; the launch traced here: 214 us
  waiting for transfers between devices  94.3 us (44%)
  Pallas kernels  59 us (27%)
  starting transfers between devices  22.4 us (10%)
  between operations  13.7 us (6%)
  blocking collectives  13.1 us (6%)
  local copies, waits for them, and re-layouts  10.8 us (5%)
    ppermute x3, waiting for transfers between devices, up(): return lax.ppermute(x, 'tm', [(i, (i + 4 * k) % devices) for i in every])  34.7 us
    ppermute x1, waiting for transfers between devices, shards(): prior = lax.ppermute(kv, 'tm', next_door)  19.8 us
    ppermute x4, waiting for transfers between devices, to_x(): return lax.ppermute(x, 'tm', across_x)  18.2 us
    ppermute x2, waiting for transfers between devices, shards(): beyond = [lax.ppermute(a, 'tm', onward) for a in beside]  13.3 us
    psum x1, blocking collectives, shards(): live_all = lax.psum(live_all, 'tm')  13.1 us
    pallas_call x1, Pallas kernels, shards(): pl.pallas_call(lambda *r: conv_kernel(plans[2], frames, *r), out_shape=li...  11.5 us
    pallas_call x1, Pallas kernels, shards(): pl.pallas_call(lambda *r: attention_kernel(frames, *r), out_shape=like((r...  11 us
    pallas_call x1, Pallas kernels, shards(): pl.pallas_call(lambda *r: gate_kernel(plans[0], plans[1], frames, *r), ou...  11 us
  transfers between devices with their start and end apart: 25, of which 13 were waited for; matrix products, arithmetic and copies ran while one was open for 3% of the time, Pallas kernels for 21%

commit v1 on v0

--- a/solution.py
+++ b/solution.py
@@ -269,7 +269,7 @@
     k, v, prior_k, prior_v = kv.at[0], kv.at[1], prior.at[0], prior.at[1]
     t = place_ref[0]
     streams = q.shape[0] // frames
-    tile = 128
+    tile = 256
     window = tile + CTX
     for s in range(streams):
         keys[pl.ds(2 * s * frames, frames)] = prior_k[pl.ds(s * frames, frames)]

time: 215 us -> 211 us (0.981)
  Pallas kernels: 59 us -> 55.3 us
    pallas_call x1, Pallas kernels: 11 us -> 7.33 us  [shards(): pl.pallas_call(lambda *r: attention_kernel(frames, *r), out_shape=like((r...]
  transfers between devices with their start and end apart: 25 -> 25, of which waited for: 13 -> 13; matrix products, arithmetic and copies ran while one was open for 3% -> 3% of each run, Pallas kernels for 21% -> 19%
where the time goes in v1:
time: 211 us; the launch traced here: 210 us
  waiting for transfers between devices  94.3 us (45%)
  Pallas kernels  55.3 us (26%)
  starting transfers between devices  22.4 us (11%)
  between operations  13.7 us (6%)
  blocking collectives  13.1 us (6%)
  local copies, waits for them, and re-layouts  10.8 us (5%)
    ppermute x3, waiting for transfers between devices, up(): return lax.ppermute(x, 'tm', [(i, (i + 4 * k) % devices) for i in every])  34.7 us
    ppermute x1, waiting for transfers between devices, shards(): prior = lax.ppermute(kv, 'tm', next_door)  19.8 us
    ppermute x4, waiting for transfers between devices, to_x(): return lax.ppermute(x, 'tm', across_x)  18.2 us
    ppermute x2, waiting for transfers between devices, shards(): beyond = [lax.ppermute(a, 'tm', onward) for a in beside]  13.3 us
    psum x1, blocking collectives, shards(): live_all = lax.psum(live_all, 'tm')  13.1 us
    pallas_call x1, Pallas kernels, shards(): pl.pallas_call(lambda *r: conv_kernel(plans[2], frames, *r), out_shape=li...  11.5 us
    pallas_call x1, Pallas kernels, shards(): pl.pallas_call(lambda *r: gate_kernel(plans[0], plans[1], frames, *r), ou...  11 us
    pallas_call x1, Pallas kernels, shards(): pl.pallas_call(lambda *r: qkv_kernel(*in_plan, *r), out_shape=[like((rows...  10.9 us
  transfers between devices with their start and end apart: 25, of which 13 were waited for; matrix products, arithmetic and copies ran while one was open for 3% of the time, Pallas kernels for 19%

profile of v1, /device:TPU:8, one launch (start us, length us, event | category | flops | bytes accessed | tf_op | source)
XLA Modules:
  0.0 210.4 jit_solution(9902676587512792315)
XLA Ops:
  7.2 3.0 %prepare.1 = (bf16[144,768]{1,0:T(8,128)(2,1)}, bf16[192,768]{1,0:T(8,128)(2,1)}, bf16[2,144,768]{2,1,0:T(8,128)(2,1)}) custom-call(s32[2]{0:T(128)} %pad_add_fusion.place_ref.r_0_, bf16[96,2304]{1,0:T(8,128)(2,1)} %w_in.1, bf16[48,1536]{1,0:T(8,128)(2,1)} %w_out.1, bf16[96,1536]{1,0:T(8,128)(2,1)} %w_expand.1, bf16[48,1536]{1,0:T(8,128)(2,1)} %w_last.1), custom_call_target="tpu_custom_call" | custom-call | tf_op jit(solution)/shard_map/prepare/pallas_call | solution.py:465
  10.3 3.4 %hand_over.1 = bf16[8,128,768]{2,1,0:T(8,128)(2,1)} custom-call(s32[2]{0:T(128)} %pad_add_fusion.place_ref.r_0_, bf16[8,128,1536]{2,1,0:T(8,128)(2,1)} %r_2_.3), custom_call_target="tpu_custom_call" | custom-call | tf_op jit(solution)/shard_map/hand_over/pallas_call | solution.py:476
  14.0 13.1 %psum.7.r_1_ = s32[128]{0:T(128)} all-reduce(s32[128]{0:T(128)S(1)} %dynamic_update_slice.3), channel_id=1, replica_groups=mesh['groups'=2,'tm'=16] {'tm'}, use_global_device_ids=true, to_apply=%region_0.1 | all-reduce | flops 128 | bytes 1024 | tf_op jit(solution)/shard_map/psum | solution.py:490
  27.6 5.4 %collective-permute-done = bf16[144,768]{1,0:T(8,128)(2,1)S(1)} collective-permute-done((bf16[144,768]{1,0:T(8,128)(2,1)S(1)}, bf16[144,768]{1,0:T(8,128)(2,1)S(1)}, u32[]{:S(2)}, u32[]{:S(2)}) %collective-permute-start) | collective-permute-done | bytes 221216 | tf_op jit(solution)/shard_map/ppermute | solution.py:448
  34.2 4.8 %route.1 = (bf16[4,128,768]{2,1,0:T(8,128)(2,1)}, bf16[4,128,768]{2,1,0:T(8,128)(2,1)}, s32[8]{0:T(128)}) custom-call(s32[2]{0:T(128)} %pad_add_fusion.place_ref.r_0_, s32[128]{0:T(128)} %psum.7.r_1_, bf16[8,128,1536]{2,1,0:T(8,128)(2,1)} %r_2_.3, bf16[8,128,768]{2,1,0:T(8,128)(2,1)} %copy-done), custom_call_target="tpu_custom_call" | custom-call | tf_op jit(solution)/shard_map/route/pallas_call | solution.py:497
  39.0 2.0 collective-permute-start.3
  41.3 3.0 %collective-permute-start.8 = (bf16[144,768]{1,0:T(8,128)(2,1)S(1)}, bf16[144,768]{1,0:T(8,128)(2,1)S(1)}, u32[]{:S(2)}, u32[]{:S(2)}) collective-permute-start(bf16[144,768]{1,0:T(8,128)(2,1)S(1)} %copy-done.17), channel_id=1, source_target_pairs={{0,8},{1,9},{2,10},{3,11},{4,12},{5,13},{6,14},{7,15},{8,0},{9,1},... | collective-permute-start | bytes 663560 | tf_op jit(solution)/shard_map/ppermute | solution.py:454
  44.3 19.3 %collective-permute-done.7 = bf16[144,768]{1,0:T(8,128)(2,1)S(1)} collective-permute-done((bf16[144,768]{1,0:T(8,128)(2,1)S(1)}, bf16[144,768]{1,0:T(8,128)(2,1)S(1)}, u32[]{:S(2)}, u32[]{:S(2)}) %collective-permute-start.7) | collective-permute-done | bytes 221216 | tf_op jit(solution)/shard_map/ppermute | solution.py:454
  63.6 12.0 %collective-permute-done.8 = bf16[144,768]{1,0:T(8,128)(2,1)S(1)} collective-permute-done((bf16[144,768]{1,0:T(8,128)(2,1)S(1)}, bf16[144,768]{1,0:T(8,128)(2,1)S(1)}, u32[]{:S(2)}, u32[]{:S(2)}) %collective-permute-start.8) | collective-permute-done | bytes 221216 | tf_op jit(solution)/shard_map/ppermute | solution.py:454
  75.6 3.4 %collective-permute-done.9 = bf16[144,768]{1,0:T(8,128)(2,1)S(1)} collective-permute-done((bf16[144,768]{1,0:T(8,128)(2,1)S(1)}, bf16[144,768]{1,0:T(8,128)(2,1)S(1)}, u32[]{:S(2)}, u32[]{:S(2)}) %collective-permute-start.9) | collective-permute-done | bytes 221216 | tf_op jit(solution)/shard_map/ppermute | solution.py:454
  83.6 4.4 %collective-permute-done.3.r_5_ = bf16[4,128,768]{2,1,0:T(8,128)(2,1)S(1)} collective-permute-done((bf16[4,128,768]{2,1,0:T(8,128)(2,1)}, bf16[4,128,768]{2,1,0:T(8,128)(2,1)S(1)}, u32[]{:S(2)}, u32[]{:S(2)}) %collective-permute-start.3) | collective-permute-done | bytes 786464 | tf_op jit(solution)/shard_map/ppermute | solution.py:448
  87.9 2.9 %collective-permute-start.5 = (bf16[4,128,768]{2,1,0:T(8,128)(2,1)S(1)}, bf16[4,128,768]{2,1,0:T(8,128)(2,1)S(1)}, u32[]{:S(2)}, u32[]{:S(2)}) collective-permute-start(bf16[4,128,768]{2,1,0:T(8,128)(2,1)S(1)} %collective-permute-done.3.r_5_), channel_id=1, source_target_pairs={{0,4},{1,5},{4,8},{5,9},{6,2},{7,3},{8,12},{9,13},{10,6},{11,7},{1... | collective-permute-start | bytes 2359304 | tf_op jit(solution)/shard_map/ppermute | solution.py:507
  90.8 8.5 %collective-permute-done.10.r_6_ = bf16[3,144,768]{2,1,0:T(8,128)(2,1)} collective-permute-done((bf16[3,144,768]{2,1,0:T(8,128)(2,1)S(1)}, bf16[3,144,768]{2,1,0:T(8,128)(2,1)}, u32[]{:S(2)}, u32[]{:S(2)}) %collective-permute-start.10) | collective-permute-done | bytes 663584 | tf_op jit(solution)/shard_map/ppermute | solution.py:448
  102.1 2.3 %collective-permute-done.11.r_7_ = bf16[4,144,768]{2,1,0:T(8,128)(2,1)S(1)} collective-permute-done((bf16[4,144,768]{2,1,0:T(8,128)(2,1)S(1)}, bf16[4,144,768]{2,1,0:T(8,128)(2,1)S(1)}, u32[]{:S(2)}, u32[]{:S(2)}) %collective-permute-start.11) | collective-permute-done | bytes 884768 | tf_op jit(solution)/shard_map/ppermute | solution.py:451
  104.4 12.3 %collective-permute-done.5.r_7_ = bf16[4,128,768]{2,1,0:T(8,128)(2,1)S(1)} collective-permute-done((bf16[4,128,768]{2,1,0:T(8,128)(2,1)S(1)}, bf16[4,128,768]{2,1,0:T(8,128)(2,1)S(1)}, u32[]{:S(2)}, u32[]{:S(2)}) %collective-permute-start.5) | collective-permute-done | bytes 786464 | tf_op jit(solution)/shard_map/ppermute | solution.py:507
  117.6 3.4 %assemble.1 = (bf16[4,128,768]{2,1,0:T(8,128)(2,1)}, bf16[4,128,768]{2,1,0:T(8,128)(2,1)}) custom-call(s32[2]{0:T(128)} %pad_add_fusion.place_ref.r_0_, s32[8]{0:T(128)} %get-tuple-element.32.r_1_, bf16[8,128,1536]{2,1,0:T(8,128)(2,1)} %r_2_.3, bf16[8,128,768]{2,1,0:T(8,128)(2,1)} %copy-done, bf16[4,128,768]{2,1,0:T(8,128)(2,1)} %copy-done.4, ...), custom_call_target="tpu_custom_call" | custom-call | tf_op jit(solution)/shard_map/assemble/pallas_call | solution.py:547
  126.0 10.9 %qkv.1 = (bf16[512,1536]{1,0:T(8,128)(2,1)}, bf16[512,768]{1,0:T(8,128)(2,1)}, bf16[2,512,768]{2,1,0:T(8,128)(2,1)}) custom-call(s32[2]{0:T(128)} %pad_add_fusion.place_ref.r_0_, bf16[4,128,768]{2,1,0:T(8,128)(2,1)} %get-tuple-element.35.r_1_, bf16[4,128,768]{2,1,0:T(8,128)(2,1)} %collective-permute-done.6.r_2_, f32[1,1536]{1,0:T(1,128)} %broadcast_in_dim.16.r_3_, ...), custom_call_target="tpu_custom_call" | custom-call | tf_op jit(solution)/shard_map/qkv/pallas_call | solution.py:558
  136.8 2.3 %collective-permute-start.18 = (bf16[2,512,768]{2,1,0:T(8,128)(2,1)}, bf16[2,512,768]{2,1,0:T(8,128)(2,1)}, u32[]{:S(2)}, u32[]{:S(2)}) collective-permute-start(bf16[2,512,768]{2,1,0:T(8,128)(2,1)} %get-tuple-element.42.r_2_), channel_id=1, source_target_pairs={{0,1},{1,2},{2,3},{3,4},{4,5},{5,6},{6,7},{7,8},{8,9},{9,10},{10,1... | collective-permute-start | bytes 4718600 | tf_op jit(solution)/shard_map/ppermute | solution.py:572
  140.0 19.8 %collective-permute-done.18.r_3_ = bf16[2,512,768]{2,1,0:T(8,128)(2,1)} collective-permute-done((bf16[2,512,768]{2,1,0:T(8,128)(2,1)}, bf16[2,512,768]{2,1,0:T(8,128)(2,1)}, u32[]{:S(2)}, u32[]{:S(2)}) %collective-permute-start.18) | collective-permute-done | bytes 1572896 | tf_op jit(solution)/shard_map/ppermute | solution.py:572
  159.8 7.3 %attention.1.r_1_ = bf16[512,768]{1,0:T(8,128)(2,1)} custom-call(s32[2]{0:T(128)} %pad_add_fusion.place_ref.r_0_, bf16[512,768]{1,0:T(8,128)(2,1)} %get-tuple-element.41.r_1_, bf16[2,512,768]{2,1,0:T(8,128)(2,1)} %get-tuple-element.42.r_2_, bf16[2,512,768]{2,1,0:T(8,128)(2,1)} %collective-permute-done.18.r_3_, s32[512,1]{1,0:T(8,128)} %bitcast.16), custom_call_target="tpu_custom_call" | custom-call | tf_op jit(solution)/shard_map/attention/pallas_call | solution.py:575
  172.3 11.0 %gate.1 = (bf16[512,1536]{1,0:T(8,128)(2,1)}, bf16[512,768]{1,0:T(8,128)(2,1)}, bf16[64,768]{1,0:T(8,128)(2,1)}) custom-call(s32[2]{0:T(128)} %pad_add_fusion.place_ref.r_0_, bf16[512,768]{1,0:T(8,128)(2,1)} %attention.1.r_1_, bf16[512,1536]{1,0:T(8,128)(2,1)} %get-tuple-element.43.r_2_, f32[1,1536]{1,0:T(1,128)} %broadcast_in_dim.18.r_3_, ...), custom_call_target="tpu_custom_call" | custom-call | tf_op jit(solution)/shard_map/gate/pallas_call | solution.py:590
  184.1 2.4 %collective-permute-start.21 = (bf16[64,768]{1,0:T(8,128)(2,1)}, bf16[64,768]{1,0:T(8,128)(2,1)S(1)}, u32[]{:S(2)}, u32[]{:S(2)}) collective-permute-start(bf16[64,768]{1,0:T(8,128)(2,1)} %get-tuple-element.48), channel_id=1, source_target_pairs={{0,1},{1,2},{2,3},{3,4},{4,5},{5,6},{6,7},{7,8},{8,9},{9,10},{10,1... | collective-permute-start | bytes 294920 | tf_op jit(solution)/shard_map/ppermute | solution.py:604
  187.1 4.0 %collective-permute-done.21.r_2_ = bf16[64,768]{1,0:T(8,128)(2,1)S(1)} collective-permute-done((bf16[64,768]{1,0:T(8,128)(2,1)}, bf16[64,768]{1,0:T(8,128)(2,1)S(1)}, u32[]{:S(2)}, u32[]{:S(2)}) %collective-permute-start.21) | collective-permute-done | bytes 98336 | tf_op jit(solution)/shard_map/ppermute | solution.py:604
  192.0 11.5 %conv.1 = bf16[512,1536]{1,0:T(8,128)(2,1)} custom-call(s32[2]{0:T(128)} %pad_add_fusion.place_ref.r_0_, bf16[512,768]{1,0:T(8,128)(2,1)} %get-tuple-element.47.r_1_, bf16[64,768]{1,0:T(8,128)(2,1)} %copy-done.12, bf16[512,1536]{1,0:T(8,128)(2,1)} %get-tuple-element.49.r_3_, s32[512,1]{1,0:T(8,128)} %bitcast.17, f32[31,768]{1,0:T(8,128)} %r_5_.1, ...), custom_call_target="tpu_custom_call" | custom-call | tf_op jit(solution)/shard_map/conv/pallas_call | solution.py:609
  (86 shorter events, 24.4 us)
Async XLA Ops:
  6.5 115.9 %all-gather.3.cloned.1.call-start = ((), (), s32[]{:S(2)}) async-start(), calls=%async_computation | async-start | bytes 5013504 | tf_op jit(solution)/shard_map/all_gather | solution.py:515
  13.7 19.4 %collective-permute-start.1 = (bf16[8,128,768]{2,1,0:T(8,128)(2,1)}, bf16[8,128,768]{2,1,0:T(8,128)(2,1)S(1)}, u32[]{:S(2)}, u32[]{:S(2)}) collective-permute-start(bf16[8,128,768]{2,1,0:T(8,128)(2,1)} %hand_over.1), channel_id=1, source_target_pairs={{0,1},{1,0},{2,3},{3,2},{4,5},{5,4},{6,7},{7,6},{8,9},{9,8},{10,11... | collective-permute-start | bytes 4718600 | tf_op jit(solution)/shard_map/ppermute | solution.py:445
  27.1 5.9 %collective-permute-start = (bf16[144,768]{1,0:T(8,128)(2,1)S(1)}, bf16[144,768]{1,0:T(8,128)(2,1)S(1)}, u32[]{:S(2)}, u32[]{:S(2)}) collective-permute-start(bf16[144,768]{1,0:T(8,128)(2,1)S(1)} %copy-done.17), channel_id=1, source_target_pairs={{0,2},{1,3},{2,0},{3,1},{4,6},{5,7},{6,4},{7,5},{8,10},{9,11},{10,... | collective-permute-start | bytes 663560 | tf_op jit(solution)/shard_map/ppermute | solution.py:448
  39.0 40.0 %collective-permute-start.2 = (bf16[4,128,768]{2,1,0:T(8,128)(2,1)}, bf16[4,128,768]{2,1,0:T(8,128)(2,1)S(1)}, u32[]{:S(2)}, u32[]{:S(2)}) collective-permute-start(bf16[4,128,768]{2,1,0:T(8,128)(2,1)} %get-tuple-element.33), channel_id=1, source_target_pairs={{0,2},{1,3},{2,0},{3,1},{4,6},{5,7},{6,4},{7,5},{8,10},{9,11},{10,... | collective-permute-start | bytes 2359304 | tf_op jit(solution)/shard_map/ppermute | solution.py:448
  39.0 48.9 %collective-permute-start.3 = (bf16[4,128,768]{2,1,0:T(8,128)(2,1)}, bf16[4,128,768]{2,1,0:T(8,128)(2,1)S(1)}, u32[]{:S(2)}, u32[]{:S(2)}) collective-permute-start(bf16[4,128,768]{2,1,0:T(8,128)(2,1)} %get-tuple-element.34), channel_id=1, source_target_pairs={{0,2},{1,3},{2,0},{3,1},{4,6},{5,7},{6,4},{7,5},{8,10},{9,11},{10,... | collective-permute-start | bytes 2359304 | tf_op jit(solution)/shard_map/ppermute | solution.py:448
  41.0 22.5 %collective-permute-start.7 = (bf16[144,768]{1,0:T(8,128)(2,1)S(1)}, bf16[144,768]{1,0:T(8,128)(2,1)S(1)}, u32[]{:S(2)}, u32[]{:S(2)}) collective-permute-start(bf16[144,768]{1,0:T(8,128)(2,1)S(1)} %copy-done.17), channel_id=1, source_target_pairs={{0,4},{1,5},{2,6},{3,7},{4,8},{5,9},{6,10},{7,11},{8,12},{9,13},{1... | collective-permute-start | bytes 663560 | tf_op jit(solution)/shard_map/ppermute | solution.py:454
  41.3 34.3 %collective-permute-start.8 = (bf16[144,768]{1,0:T(8,128)(2,1)S(1)}, bf16[144,768]{1,0:T(8,128)(2,1)S(1)}, u32[]{:S(2)}, u32[]{:S(2)}) collective-permute-start(bf16[144,768]{1,0:T(8,128)(2,1)S(1)} %copy-done.17), channel_id=1, source_target_pairs={{0,8},{1,9},{2,10},{3,11},{4,12},{5,13},{6,14},{7,15},{8,0},{9,1},... | collective-permute-start | bytes 663560 | tf_op jit(solution)/shard_map/ppermute | solution.py:454
  44.3 34.7 %collective-permute-start.9 = (bf16[144,768]{1,0:T(8,128)(2,1)S(1)}, bf16[144,768]{1,0:T(8,128)(2,1)S(1)}, u32[]{:S(2)}, u32[]{:S(2)}) collective-permute-start(bf16[144,768]{1,0:T(8,128)(2,1)S(1)} %copy-done.17), channel_id=1, source_target_pairs={{0,12},{1,13},{2,14},{3,15},{4,0},{5,1},{6,2},{7,3},{8,4},{9,5},{1... | collective-permute-start | bytes 663560 | tf_op jit(solution)/shard_map/ppermute | solution.py:454
  79.1 20.2 %collective-permute-start.10 = (bf16[3,144,768]{2,1,0:T(8,128)(2,1)S(1)}, bf16[3,144,768]{2,1,0:T(8,128)(2,1)}, u32[]{:S(2)}, u32[]{:S(2)}) collective-permute-start(bf16[3,144,768]{2,1,0:T(8,128)(2,1)S(1)} %pad_maximum_fusion.1), channel_id=1, source_target_pairs={{0,2},{1,3},{2,0},{3,1},{4,6},{5,7},{6,4},{7,5},{8,10},{9,11},{10,... | collective-permute-start | bytes 1990664 | tf_op jit(solution)/shard_map/ppermute | solution.py:448
  79.7 22.4 %collective-permute-start.4 = (bf16[4,128,768]{2,1,0:T(8,128)(2,1)S(1)}, bf16[4,128,768]{2,1,0:T(8,128)(2,1)S(1)}, u32[]{:S(2)}, u32[]{:S(2)}) collective-permute-start(bf16[4,128,768]{2,1,0:T(8,128)(2,1)S(1)} %collective-permute-done.2.r_4_), channel_id=1, source_target_pairs={{0,4},{1,5},{4,8},{5,9},{6,2},{7,3},{8,12},{9,13},{10,6},{11,7},{1... | collective-permute-start | bytes 2359304 | tf_op jit(solution)/shard_map/ppermute | solution.py:507
  81.7 22.6 %collective-permute-start.11 = (bf16[4,144,768]{2,1,0:T(8,128)(2,1)S(1)}, bf16[4,144,768]{2,1,0:T(8,128)(2,1)S(1)}, u32[]{:S(2)}, u32[]{:S(2)}) collective-permute-start(bf16[4,144,768]{2,1,0:T(8,128)(2,1)S(1)} %pad_maximum_fusion.r_5_), channel_id=1, source_target_pairs={{0,16},{16,0},{1,17},{17,1},{2,18},{18,2},{3,19},{19,3},{4,20},{20... | collective-permute-start | bytes 2654216 | tf_op jit(solution)/shard_map/ppermute | solution.py:451
  87.9 28.7 %collective-permute-start.5 = (bf16[4,128,768]{2,1,0:T(8,128)(2,1)S(1)}, bf16[4,128,768]{2,1,0:T(8,128)(2,1)S(1)}, u32[]{:S(2)}, u32[]{:S(2)}) collective-permute-start(bf16[4,128,768]{2,1,0:T(8,128)(2,1)S(1)} %collective-permute-done.3.r_5_), channel_id=1, source_target_pairs={{0,4},{1,5},{4,8},{5,9},{6,2},{7,3},{8,12},{9,13},{10,6},{11,7},{1... | collective-permute-start | bytes 2359304 | tf_op jit(solution)/shard_map/ppermute | solution.py:507
  99.3 23.2 %collective-permute-start.12 = (bf16[3,144,768]{2,1,0:T(8,128)(2,1)}, bf16[3,144,768]{2,1,0:T(8,128)(2,1)}, u32[]{:S(2)}, u32[]{:S(2)}) collective-permute-start(bf16[3,144,768]{2,1,0:T(8,128)(2,1)} %collective-permute-done.10.r_6_), channel_id=1, source_target_pairs={{0,16},{16,0},{1,17},{17,1},{2,18},{18,2},{3,19},{19,3},{4,20},{20... | collective-permute-start | bytes 1990664 | tf_op jit(solution)/shard_map/ppermute | solution.py:451
  101.0 20.1 %collective-permute-start.13 = (bf16[2,144,768]{2,1,0:T(8,128)(2,1)S(1)}, bf16[2,144,768]{2,1,0:T(8,128)(2,1)S(1)}, u32[]{:S(2)}, u32[]{:S(2)}) collective-permute-start(bf16[2,144,768]{2,1,0:T(8,128)(2,1)S(1)} %copy-done.10), channel_id=1, source_target_pairs={{0,1},{1,0},{2,3},{3,2},{4,5},{5,4},{6,7},{7,6},{8,9},{9,8},{10,11... | collective-permute-start | bytes 1327112 | tf_op jit(solution)/shard_map/ppermute | solution.py:445
  102.1 22.1 %collective-permute-start.14 = (bf16[4,144,768]{2,1,0:T(8,128)(2,1)S(1)}, bf16[4,144,768]{2,1,0:T(8,128)(2,1)}, u32[]{:S(2)}, u32[]{:S(2)}) collective-permute-start(bf16[4,144,768]{2,1,0:T(8,128)(2,1)S(1)} %pad_maximum_fusion.r_5_), channel_id=1, source_target_pairs={{0,1},{1,0},{2,3},{3,2},{4,5},{5,4},{6,7},{7,6},{8,9},{9,8},{10,11... | collective-permute-start | bytes 2654216 | tf_op jit(solution)/shard_map/ppermute | solution.py:445
  104.4 21.6 %collective-permute-start.16 = (bf16[4,144,768]{2,1,0:T(8,128)(2,1)S(1)}, bf16[4,144,768]{2,1,0:T(8,128)(2,1)}, u32[]{:S(2)}, u32[]{:S(2)}) collective-permute-start(bf16[4,144,768]{2,1,0:T(8,128)(2,1)S(1)} %collective-permute-done.11.r_7_), channel_id=1, source_target_pairs={{0,1},{1,0},{2,3},{3,2},{4,5},{5,4},{6,7},{7,6},{8,9},{9,8},{10,11... | collective-permute-start | bytes 2654216 | tf_op jit(solution)/shard_map/ppermute | solution.py:445
  121.1 4.9 %collective-permute-start.6 = (bf16[4,128,768]{2,1,0:T(8,128)(2,1)}, bf16[4,128,768]{2,1,0:T(8,128)(2,1)}, u32[]{:S(2)}, u32[]{:S(2)}) collective-permute-start(bf16[4,128,768]{2,1,0:T(8,128)(2,1)} %get-tuple-element.36), channel_id=1, source_target_pairs={{0,1},{1,0},{2,3},{3,2},{4,5},{5,4},{6,7},{7,6},{8,9},{9,8},{10,11... | collective-permute-start | bytes 2359304 | tf_op jit(solution)/shard_map/ppermute | solution.py:445
  121.9 4.0 %collective-permute-start.15 = (bf16[3,144,768]{2,1,0:T(8,128)(2,1)}, bf16[3,144,768]{2,1,0:T(8,128)(2,1)}, u32[]{:S(2)}, u32[]{:S(2)}) collective-permute-start(bf16[3,144,768]{2,1,0:T(8,128)(2,1)} %collective-permute-done.10.r_6_), channel_id=1, source_target_pairs={{0,1},{1,0},{2,3},{3,2},{4,5},{5,4},{6,7},{7,6},{8,9},{9,8},{10,11... | collective-permute-start | bytes 1990664 | tf_op jit(solution)/shard_map/ppermute | solution.py:445
  124.2 43.0 %collective-permute-start.19 = (bf16[16,144,384]{2,1,0:T(8,128)(2,1)S(1)}, bf16[16,144,384]{2,1,0:T(8,128)(2,1)}, u32[]{:S(2)}, u32[]{:S(2)}) collective-permute-start(bf16[16,144,384]{2,1,0:T(8,128)(2,1)S(1)} %constant_dynamic-slice_fusion.1), channel_id=1, source_target_pairs={{0,16},{16,0},{1,17},{17,1},{2,18},{18,2},{3,19},{19,3},{4,20},{20... | collective-permute-start | bytes 5308424 | tf_op jit(solution)/shard_map/ppermute | solution.py:451
  136.8 23.0 %collective-permute-start.18 = (bf16[2,512,768]{2,1,0:T(8,128)(2,1)}, bf16[2,512,768]{2,1,0:T(8,128)(2,1)}, u32[]{:S(2)}, u32[]{:S(2)}) collective-permute-start(bf16[2,512,768]{2,1,0:T(8,128)(2,1)} %get-tuple-element.42.r_2_), channel_id=1, source_target_pairs={{0,1},{1,2},{2,3},{3,4},{4,5},{5,6},{6,7},{7,8},{8,9},{9,10},{10,1... | collective-permute-start | bytes 4718600 | tf_op jit(solution)/shard_map/ppermute | solution.py:572
  167.1 3.9 %collective-permute-start.20 = (bf16[16,144,384]{2,1,0:T(8,128)(2,1)}, bf16[16,144,384]{2,1,0:T(8,128)(2,1)S(1)}, u32[]{:S(2)}, u32[]{:S(2)}) collective-permute-start(bf16[16,144,384]{2,1,0:T(8,128)(2,1)} %collective-permute-done.19.r_5_), channel_id=1, source_target_pairs={{0,1},{1,0},{2,3},{3,2},{4,5},{5,4},{6,7},{7,6},{8,9},{9,8},{10,11... | collective-permute-start | bytes 5308424 | tf_op jit(solution)/shard_map/ppermute | solution.py:445
  168.3 15.8 %collective-permute-start.22 = (bf16[16,48,384]{2,1,0:T(8,128)(2,1)S(1)}, bf16[16,48,384]{2,1,0:T(8,128)(2,1)S(1)}, u32[]{:S(2)}, u32[]{:S(2)}) collective-permute-start(bf16[16,48,384]{2,1,0:T(8,128)(2,1)S(1)} %constant_dynamic-slice_fusion), channel_id=1, source_target_pairs={{0,16},{16,0},{1,17},{17,1},{2,18},{18,2},{3,19},{19,3},{4,20},{20... | collective-permute-start | bytes 1769480 | tf_op jit(solution)/shard_map/ppermute | solution.py:451
  184.1 7.0 %collective-permute-start.23 = (bf16[16,48,384]{2,1,0:T(8,128)(2,1)S(1)}, bf16[16,48,384]{2,1,0:T(8,128)(2,1)S(1)}, u32[]{:S(2)}, u32[]{:S(2)}) collective-permute-start(bf16[16,48,384]{2,1,0:T(8,128)(2,1)S(1)} %collective-permute-done.22.r_8_), channel_id=1, source_target_pairs={{0,1},{1,0},{2,3},{3,2},{4,5},{5,4},{6,7},{7,6},{8,9},{9,8},{10,11... | collective-permute-start | bytes 1769480 | tf_op jit(solution)/shard_map/ppermute | solution.py:445
  184.1 7.0 %collective-permute-start.21 = (bf16[64,768]{1,0:T(8,128)(2,1)}, bf16[64,768]{1,0:T(8,128)(2,1)S(1)}, u32[]{:S(2)}, u32[]{:S(2)}) collective-permute-start(bf16[64,768]{1,0:T(8,128)(2,1)} %get-tuple-element.48), channel_id=1, source_target_pairs={{0,1},{1,2},{2,3},{3,4},{4,5},{5,6},{6,7},{7,8},{8,9},{9,10},{10,1... | collective-permute-start | bytes 294920 | tf_op jit(solution)/shard_map/ppermute | solution.py:604
  (20 other events, 275.4 us)
Sparse Core Ops, SparseCore 0:
  10.4 67.3 all-gather.2

commit v2 on v1

--- a/solution.py
+++ b/solution.py
@@ -315,7 +315,7 @@
             mixed[here, pl.ds(base + 256, 128)] = jnp.where(lane < 32, outs[2][:, 128:], outs[3]).astype(bf16)
         return carry
 
-    lax.fori_loop(0, streams * tiles, body, 0)
+    lax.fori_loop(0, streams * tiles, body, 0, unroll=True)
 
 
 def gate_kernel(out_plan, in_plan, frames, place_ref, mixed, stream, gain, *rest):

time: 211 us -> 211 us (level)
  no operation moved by 1% of the time
where the time goes in v2:
time: 211 us; the launch traced here: 210 us
  waiting for transfers between devices  94.3 us (45%)
  Pallas kernels  55 us (26%)
  starting transfers between devices  22.4 us (11%)
  between operations  13.7 us (6%)
  blocking collectives  13.1 us (6%)
  local copies, waits for them, and re-layouts  10.8 us (5%)
    ppermute x3, waiting for transfers between devices, up(): return lax.ppermute(x, 'tm', [(i, (i + 4 * k) % devices) for i in every])  34.7 us
    ppermute x1, waiting for transfers between devices, shards(): prior = lax.ppermute(kv, 'tm', next_door)  19.8 us
    ppermute x4, waiting for transfers between devices, to_x(): return lax.ppermute(x, 'tm', across_x)  18.2 us
    ppermute x2, waiting for transfers between devices, shards(): beyond = [lax.ppermute(a, 'tm', onward) for a in beside]  13.3 us
    psum x1, blocking collectives, shards(): live_all = lax.psum(live_all, 'tm')  13.1 us
    pallas_call x1, Pallas kernels, shards(): pl.pallas_call(lambda *r: conv_kernel(plans[2], frames, *r), out_shape=li...  11.5 us
    pallas_call x1, Pallas kernels, shards(): pl.pallas_call(lambda *r: gate_kernel(plans[0], plans[1], frames, *r), ou...  11 us
    pallas_call x1, Pallas kernels, shards(): pl.pallas_call(lambda *r: qkv_kernel(*in_plan, *r), out_shape=[like((rows...  10.9 us
  transfers between devices with their start and end apart: 25, of which 13 were waited for; matrix products, arithmetic and copies ran while one was open for 3% of the time, Pallas kernels for 19%

profile of v2, /device:TPU:8, one launch (start us, length us, event | category | flops | bytes accessed | tf_op | source)
XLA Modules:
  0.0 210.1 jit_solution(16842461744638690114)
XLA Ops:
  7.2 3.0 %prepare.1 = (bf16[144,768]{1,0:T(8,128)(2,1)}, bf16[192,768]{1,0:T(8,128)(2,1)}, bf16[2,144,768]{2,1,0:T(8,128)(2,1)}) custom-call(s32[2]{0:T(128)} %pad_add_fusion.place_ref.r_0_, bf16[96,2304]{1,0:T(8,128)(2,1)} %w_in.1, bf16[48,1536]{1,0:T(8,128)(2,1)} %w_out.1, bf16[96,1536]{1,0:T(8,128)(2,1)} %w_expand.1, bf16[48,1536]{1,0:T(8,128)(2,1)} %w_last.1), custom_call_target="tpu_custom_call" | custom-call | tf_op jit(solution)/shard_map/prepare/pallas_call | solution.py:465
  10.3 3.4 %hand_over.1 = bf16[8,128,768]{2,1,0:T(8,128)(2,1)} custom-call(s32[2]{0:T(128)} %pad_add_fusion.place_ref.r_0_, bf16[8,128,1536]{2,1,0:T(8,128)(2,1)} %r_2_.3), custom_call_target="tpu_custom_call" | custom-call | tf_op jit(solution)/shard_map/hand_over/pallas_call | solution.py:476
  14.0 13.1 %psum.7.r_1_ = s32[128]{0:T(128)} all-reduce(s32[128]{0:T(128)S(1)} %dynamic_update_slice.3), channel_id=1, replica_groups=mesh['groups'=2,'tm'=16] {'tm'}, use_global_device_ids=true, to_apply=%region_0.1 | all-reduce | flops 128 | bytes 1024 | tf_op jit(solution)/shard_map/psum | solution.py:490
  27.6 5.4 %collective-permute-done = bf16[144,768]{1,0:T(8,128)(2,1)S(1)} collective-permute-done((bf16[144,768]{1,0:T(8,128)(2,1)S(1)}, bf16[144,768]{1,0:T(8,128)(2,1)S(1)}, u32[]{:S(2)}, u32[]{:S(2)}) %collective-permute-start) | collective-permute-done | bytes 221216 | tf_op jit(solution)/shard_map/ppermute | solution.py:448
  34.2 4.8 %route.1 = (bf16[4,128,768]{2,1,0:T(8,128)(2,1)}, bf16[4,128,768]{2,1,0:T(8,128)(2,1)}, s32[8]{0:T(128)}) custom-call(s32[2]{0:T(128)} %pad_add_fusion.place_ref.r_0_, s32[128]{0:T(128)} %psum.7.r_1_, bf16[8,128,1536]{2,1,0:T(8,128)(2,1)} %r_2_.3, bf16[8,128,768]{2,1,0:T(8,128)(2,1)} %copy-done), custom_call_target="tpu_custom_call" | custom-call | tf_op jit(solution)/shard_map/route/pallas_call | solution.py:497
  39.0 2.0 collective-permute-start.3
  41.1 3.2 %collective-permute-start.8 = (bf16[144,768]{1,0:T(8,128)(2,1)S(1)}, bf16[144,768]{1,0:T(8,128)(2,1)S(1)}, u32[]{:S(2)}, u32[]{:S(2)}) collective-permute-start(bf16[144,768]{1,0:T(8,128)(2,1)S(1)} %copy-done.17), channel_id=1, source_target_pairs={{0,8},{1,9},{2,10},{3,11},{4,12},{5,13},{6,14},{7,15},{8,0},{9,1},... | collective-permute-start | bytes 663560 | tf_op jit(solution)/shard_map/ppermute | solution.py:454
  44.3 19.2 %collective-permute-done.7 = bf16[144,768]{1,0:T(8,128)(2,1)S(1)} collective-permute-done((bf16[144,768]{1,0:T(8,128)(2,1)S(1)}, bf16[144,768]{1,0:T(8,128)(2,1)S(1)}, u32[]{:S(2)}, u32[]{:S(2)}) %collective-permute-start.7) | collective-permute-done | bytes 221216 | tf_op jit(solution)/shard_map/ppermute | solution.py:454
  63.4 12.1 %collective-permute-done.8 = bf16[144,768]{1,0:T(8,128)(2,1)S(1)} collective-permute-done((bf16[144,768]{1,0:T(8,128)(2,1)S(1)}, bf16[144,768]{1,0:T(8,128)(2,1)S(1)}, u32[]{:S(2)}, u32[]{:S(2)}) %collective-permute-start.8) | collective-permute-done | bytes 221216 | tf_op jit(solution)/shard_map/ppermute | solution.py:454
  75.6 3.4 %collective-permute-done.9 = bf16[144,768]{1,0:T(8,128)(2,1)S(1)} collective-permute-done((bf16[144,768]{1,0:T(8,128)(2,1)S(1)}, bf16[144,768]{1,0:T(8,128)(2,1)S(1)}, u32[]{:S(2)}, u32[]{:S(2)}) %collective-permute-start.9) | collective-permute-done | bytes 221216 | tf_op jit(solution)/shard_map/ppermute | solution.py:454
  83.6 4.4 %collective-permute-done.3.r_5_ = bf16[4,128,768]{2,1,0:T(8,128)(2,1)S(1)} collective-permute-done((bf16[4,128,768]{2,1,0:T(8,128)(2,1)}, bf16[4,128,768]{2,1,0:T(8,128)(2,1)S(1)}, u32[]{:S(2)}, u32[]{:S(2)}) %collective-permute-start.3) | collective-permute-done | bytes 786464 | tf_op jit(solution)/shard_map/ppermute | solution.py:448
  87.9 2.9 %collective-permute-start.5 = (bf16[4,128,768]{2,1,0:T(8,128)(2,1)S(1)}, bf16[4,128,768]{2,1,0:T(8,128)(2,1)S(1)}, u32[]{:S(2)}, u32[]{:S(2)}) collective-permute-start(bf16[4,128,768]{2,1,0:T(8,128)(2,1)S(1)} %collective-permute-done.3.r_5_), channel_id=1, source_target_pairs={{0,4},{1,5},{4,8},{5,9},{6,2},{7,3},{8,12},{9,13},{10,6},{11,7},{1... | collective-permute-start | bytes 2359304 | tf_op jit(solution)/shard_map/ppermute | solution.py:507
  90.8 8.5 %collective-permute-done.10.r_6_ = bf16[3,144,768]{2,1,0:T(8,128)(2,1)} collective-permute-done((bf16[3,144,768]{2,1,0:T(8,128)(2,1)S(1)}, bf16[3,144,768]{2,1,0:T(8,128)(2,1)}, u32[]{:S(2)}, u32[]{:S(2)}) %collective-permute-start.10) | collective-permute-done | bytes 663584 | tf_op jit(solution)/shard_map/ppermute | solution.py:448
  102.1 2.3 %collective-permute-done.11.r_7_ = bf16[4,144,768]{2,1,0:T(8,128)(2,1)S(1)} collective-permute-done((bf16[4,144,768]{2,1,0:T(8,128)(2,1)S(1)}, bf16[4,144,768]{2,1,0:T(8,128)(2,1)S(1)}, u32[]{:S(2)}, u32[]{:S(2)}) %collective-permute-start.11) | collective-permute-done | bytes 884768 | tf_op jit(solution)/shard_map/ppermute | solution.py:451
  104.4 12.3 %collective-permute-done.5.r_7_ = bf16[4,128,768]{2,1,0:T(8,128)(2,1)S(1)} collective-permute-done((bf16[4,128,768]{2,1,0:T(8,128)(2,1)S(1)}, bf16[4,128,768]{2,1,0:T(8,128)(2,1)S(1)}, u32[]{:S(2)}, u32[]{:S(2)}) %collective-permute-start.5) | collective-permute-done | bytes 786464 | tf_op jit(solution)/shard_map/ppermute | solution.py:507
  117.6 3.4 %assemble.1 = (bf16[4,128,768]{2,1,0:T(8,128)(2,1)}, bf16[4,128,768]{2,1,0:T(8,128)(2,1)}) custom-call(s32[2]{0:T(128)} %pad_add_fusion.place_ref.r_0_, s32[8]{0:T(128)} %get-tuple-element.32.r_1_, bf16[8,128,1536]{2,1,0:T(8,128)(2,1)} %r_2_.3, bf16[8,128,768]{2,1,0:T(8,128)(2,1)} %copy-done, bf16[4,128,768]{2,1,0:T(8,128)(2,1)} %copy-done.4, ...), custom_call_target="tpu_custom_call" | custom-call | tf_op jit(solution)/shard_map/assemble/pallas_call | solution.py:547
  126.0 10.9 %qkv.1 = (bf16[512,1536]{1,0:T(8,128)(2,1)}, bf16[512,768]{1,0:T(8,128)(2,1)}, bf16[2,512,768]{2,1,0:T(8,128)(2,1)}) custom-call(s32[2]{0:T(128)} %pad_add_fusion.place_ref.r_0_, bf16[4,128,768]{2,1,0:T(8,128)(2,1)} %get-tuple-element.35.r_1_, bf16[4,128,768]{2,1,0:T(8,128)(2,1)} %collective-permute-done.6.r_2_, f32[1,1536]{1,0:T(1,128)} %broadcast_in_dim.16.r_3_, ...), custom_call_target="tpu_custom_call" | custom-call | tf_op jit(solution)/shard_map/qkv/pallas_call | solution.py:558
  136.8 2.3 %collective-permute-start.18 = (bf16[2,512,768]{2,1,0:T(8,128)(2,1)}, bf16[2,512,768]{2,1,0:T(8,128)(2,1)}, u32[]{:S(2)}, u32[]{:S(2)}) collective-permute-start(bf16[2,512,768]{2,1,0:T(8,128)(2,1)} %get-tuple-element.42.r_2_), channel_id=1, source_target_pairs={{0,1},{1,2},{2,3},{3,4},{4,5},{5,6},{6,7},{7,8},{8,9},{9,10},{10,1... | collective-permute-start | bytes 4718600 | tf_op jit(solution)/shard_map/ppermute | solution.py:572
  140.0 19.8 %collective-permute-done.18.r_3_ = bf16[2,512,768]{2,1,0:T(8,128)(2,1)} collective-permute-done((bf16[2,512,768]{2,1,0:T(8,128)(2,1)}, bf16[2,512,768]{2,1,0:T(8,128)(2,1)}, u32[]{:S(2)}, u32[]{:S(2)}) %collective-permute-start.18) | collective-permute-done | bytes 1572896 | tf_op jit(solution)/shard_map/ppermute | solution.py:572
  159.8 7.1 %attention.1.r_1_ = bf16[512,768]{1,0:T(8,128)(2,1)} custom-call(s32[2]{0:T(128)} %pad_add_fusion.place_ref.r_0_, bf16[512,768]{1,0:T(8,128)(2,1)} %get-tuple-element.41.r_1_, bf16[2,512,768]{2,1,0:T(8,128)(2,1)} %get-tuple-element.42.r_2_, bf16[2,512,768]{2,1,0:T(8,128)(2,1)} %collective-permute-done.18.r_3_, s32[512,1]{1,0:T(8,128)} %bitcast.16), custom_call_target="tpu_custom_call" | custom-call | tf_op jit(solution)/shard_map/attention/pallas_call | solution.py:575
  172.1 11.0 %gate.1 = (bf16[512,1536]{1,0:T(8,128)(2,1)}, bf16[512,768]{1,0:T(8,128)(2,1)}, bf16[64,768]{1,0:T(8,128)(2,1)}) custom-call(s32[2]{0:T(128)} %pad_add_fusion.place_ref.r_0_, bf16[512,768]{1,0:T(8,128)(2,1)} %attention.1.r_1_, bf16[512,1536]{1,0:T(8,128)(2,1)} %get-tuple-element.43.r_2_, f32[1,1536]{1,0:T(1,128)} %broadcast_in_dim.18.r_3_, ...), custom_call_target="tpu_custom_call" | custom-call | tf_op jit(solution)/shard_map/gate/pallas_call | solution.py:590
  183.8 2.4 %collective-permute-start.21 = (bf16[64,768]{1,0:T(8,128)(2,1)}, bf16[64,768]{1,0:T(8,128)(2,1)S(1)}, u32[]{:S(2)}, u32[]{:S(2)}) collective-permute-start(bf16[64,768]{1,0:T(8,128)(2,1)} %get-tuple-element.48), channel_id=1, source_target_pairs={{0,1},{1,2},{2,3},{3,4},{4,5},{5,6},{6,7},{7,8},{8,9},{9,10},{10,1... | collective-permute-start | bytes 294920 | tf_op jit(solution)/shard_map/ppermute | solution.py:604
  186.9 4.0 %collective-permute-done.21.r_2_ = bf16[64,768]{1,0:T(8,128)(2,1)S(1)} collective-permute-done((bf16[64,768]{1,0:T(8,128)(2,1)}, bf16[64,768]{1,0:T(8,128)(2,1)S(1)}, u32[]{:S(2)}, u32[]{:S(2)}) %collective-permute-start.21) | collective-permute-done | bytes 98336 | tf_op jit(solution)/shard_map/ppermute | solution.py:604
  191.7 11.5 %conv.1 = bf16[512,1536]{1,0:T(8,128)(2,1)} custom-call(s32[2]{0:T(128)} %pad_add_fusion.place_ref.r_0_, bf16[512,768]{1,0:T(8,128)(2,1)} %get-tuple-element.47.r_1_, bf16[64,768]{1,0:T(8,128)(2,1)} %copy-done.12, bf16[512,1536]{1,0:T(8,128)(2,1)} %get-tuple-element.49.r_3_, s32[512,1]{1,0:T(8,128)} %bitcast.17, f32[31,768]{1,0:T(8,128)} %r_5_.1, ...), custom_call_target="tpu_custom_call" | custom-call | tf_op jit(solution)/shard_map/conv/pallas_call | solution.py:609
  (86 shorter events, 24.2 us)
Async XLA Ops:
  6.5 115.9 %all-gather.3.cloned.1.call-start = ((), (), s32[]{:S(2)}) async-start(), calls=%async_computation | async-start | bytes 5013504 | tf_op jit(solution)/shard_map/all_gather | solution.py:515
  13.7 19.4 %collective-permute-start.1 = (bf16[8,128,768]{2,1,0:T(8,128)(2,1)}, bf16[8,128,768]{2,1,0:T(8,128)(2,1)S(1)}, u32[]{:S(2)}, u32[]{:S(2)}) collective-permute-start(bf16[8,128,768]{2,1,0:T(8,128)(2,1)} %hand_over.1), channel_id=1, source_target_pairs={{0,1},{1,0},{2,3},{3,2},{4,5},{5,4},{6,7},{7,6},{8,9},{9,8},{10,11... | collective-permute-start | bytes 4718600 | tf_op jit(solution)/shard_map/ppermute | solution.py:445
  27.1 5.9 %collective-permute-start = (bf16[144,768]{1,0:T(8,128)(2,1)S(1)}, bf16[144,768]{1,0:T(8,128)(2,1)S(1)}, u32[]{:S(2)}, u32[]{:S(2)}) collective-permute-start(bf16[144,768]{1,0:T(8,128)(2,1)S(1)} %copy-done.17), channel_id=1, source_target_pairs={{0,2},{1,3},{2,0},{3,1},{4,6},{5,7},{6,4},{7,5},{8,10},{9,11},{10,... | collective-permute-start | bytes 663560 | tf_op jit(solution)/shard_map/ppermute | solution.py:448
  39.0 40.0 %collective-permute-start.2 = (bf16[4,128,768]{2,1,0:T(8,128)(2,1)}, bf16[4,128,768]{2,1,0:T(8,128)(2,1)S(1)}, u32[]{:S(2)}, u32[]{:S(2)}) collective-permute-start(bf16[4,128,768]{2,1,0:T(8,128)(2,1)} %get-tuple-element.33), channel_id=1, source_target_pairs={{0,2},{1,3},{2,0},{3,1},{4,6},{5,7},{6,4},{7,5},{8,10},{9,11},{10,... | collective-permute-start | bytes 2359304 | tf_op jit(solution)/shard_map/ppermute | solution.py:448
  39.0 48.9 %collective-permute-start.3 = (bf16[4,128,768]{2,1,0:T(8,128)(2,1)}, bf16[4,128,768]{2,1,0:T(8,128)(2,1)S(1)}, u32[]{:S(2)}, u32[]{:S(2)}) collective-permute-start(bf16[4,128,768]{2,1,0:T(8,128)(2,1)} %get-tuple-element.34), channel_id=1, source_target_pairs={{0,2},{1,3},{2,0},{3,1},{4,6},{5,7},{6,4},{7,5},{8,10},{9,11},{10,... | collective-permute-start | bytes 2359304 | tf_op jit(solution)/shard_map/ppermute | solution.py:448
  41.0 22.4 %collective-permute-start.7 = (bf16[144,768]{1,0:T(8,128)(2,1)S(1)}, bf16[144,768]{1,0:T(8,128)(2,1)S(1)}, u32[]{:S(2)}, u32[]{:S(2)}) collective-permute-start(bf16[144,768]{1,0:T(8,128)(2,1)S(1)} %copy-done.17), channel_id=1, source_target_pairs={{0,4},{1,5},{2,6},{3,7},{4,8},{5,9},{6,10},{7,11},{8,12},{9,13},{1... | collective-permute-start | bytes 663560 | tf_op jit(solution)/shard_map/ppermute | solution.py:454
  41.1 34.5 %collective-permute-start.8 = (bf16[144,768]{1,0:T(8,128)(2,1)S(1)}, bf16[144,768]{1,0:T(8,128)(2,1)S(1)}, u32[]{:S(2)}, u32[]{:S(2)}) collective-permute-start(bf16[144,768]{1,0:T(8,128)(2,1)S(1)} %copy-done.17), channel_id=1, source_target_pairs={{0,8},{1,9},{2,10},{3,11},{4,12},{5,13},{6,14},{7,15},{8,0},{9,1},... | collective-permute-start | bytes 663560 | tf_op jit(solution)/shard_map/ppermute | solution.py:454
  44.3 34.7 %collective-permute-start.9 = (bf16[144,768]{1,0:T(8,128)(2,1)S(1)}, bf16[144,768]{1,0:T(8,128)(2,1)S(1)}, u32[]{:S(2)}, u32[]{:S(2)}) collective-permute-start(bf16[144,768]{1,0:T(8,128)(2,1)S(1)} %copy-done.17), channel_id=1, source_target_pairs={{0,12},{1,13},{2,14},{3,15},{4,0},{5,1},{6,2},{7,3},{8,4},{9,5},{1... | collective-permute-start | bytes 663560 | tf_op jit(solution)/shard_map/ppermute | solution.py:454
  79.1 20.2 %collective-permute-start.10 = (bf16[3,144,768]{2,1,0:T(8,128)(2,1)S(1)}, bf16[3,144,768]{2,1,0:T(8,128)(2,1)}, u32[]{:S(2)}, u32[]{:S(2)}) collective-permute-start(bf16[3,144,768]{2,1,0:T(8,128)(2,1)S(1)} %pad_maximum_fusion.1), channel_id=1, source_target_pairs={{0,2},{1,3},{2,0},{3,1},{4,6},{5,7},{6,4},{7,5},{8,10},{9,11},{10,... | collective-permute-start | bytes 1990664 | tf_op jit(solution)/shard_map/ppermute | solution.py:448
  79.7 22.4 %collective-permute-start.4 = (bf16[4,128,768]{2,1,0:T(8,128)(2,1)S(1)}, bf16[4,128,768]{2,1,0:T(8,128)(2,1)S(1)}, u32[]{:S(2)}, u32[]{:S(2)}) collective-permute-start(bf16[4,128,768]{2,1,0:T(8,128)(2,1)S(1)} %collective-permute-done.2.r_4_), channel_id=1, source_target_pairs={{0,4},{1,5},{4,8},{5,9},{6,2},{7,3},{8,12},{9,13},{10,6},{11,7},{1... | collective-permute-start | bytes 2359304 | tf_op jit(solution)/shard_map/ppermute | solution.py:507
  81.7 22.6 %collective-permute-start.11 = (bf16[4,144,768]{2,1,0:T(8,128)(2,1)S(1)}, bf16[4,144,768]{2,1,0:T(8,128)(2,1)S(1)}, u32[]{:S(2)}, u32[]{:S(2)}) collective-permute-start(bf16[4,144,768]{2,1,0:T(8,128)(2,1)S(1)} %pad_maximum_fusion.r_5_), channel_id=1, source_target_pairs={{0,16},{16,0},{1,17},{17,1},{2,18},{18,2},{3,19},{19,3},{4,20},{20... | collective-permute-start | bytes 2654216 | tf_op jit(solution)/shard_map/ppermute | solution.py:451
  87.9 28.7 %collective-permute-start.5 = (bf16[4,128,768]{2,1,0:T(8,128)(2,1)S(1)}, bf16[4,128,768]{2,1,0:T(8,128)(2,1)S(1)}, u32[]{:S(2)}, u32[]{:S(2)}) collective-permute-start(bf16[4,128,768]{2,1,0:T(8,128)(2,1)S(1)} %collective-permute-done.3.r_5_), channel_id=1, source_target_pairs={{0,4},{1,5},{4,8},{5,9},{6,2},{7,3},{8,12},{9,13},{10,6},{11,7},{1... | collective-permute-start | bytes 2359304 | tf_op jit(solution)/shard_map/ppermute | solution.py:507
  99.3 23.2 %collective-permute-start.12 = (bf16[3,144,768]{2,1,0:T(8,128)(2,1)}, bf16[3,144,768]{2,1,0:T(8,128)(2,1)}, u32[]{:S(2)}, u32[]{:S(2)}) collective-permute-start(bf16[3,144,768]{2,1,0:T(8,128)(2,1)} %collective-permute-done.10.r_6_), channel_id=1, source_target_pairs={{0,16},{16,0},{1,17},{17,1},{2,18},{18,2},{3,19},{19,3},{4,20},{20... | collective-permute-start | bytes 1990664 | tf_op jit(solution)/shard_map/ppermute | solution.py:451
  101.0 20.1 %collective-permute-start.13 = (bf16[2,144,768]{2,1,0:T(8,128)(2,1)S(1)}, bf16[2,144,768]{2,1,0:T(8,128)(2,1)S(1)}, u32[]{:S(2)}, u32[]{:S(2)}) collective-permute-start(bf16[2,144,768]{2,1,0:T(8,128)(2,1)S(1)} %copy-done.10), channel_id=1, source_target_pairs={{0,1},{1,0},{2,3},{3,2},{4,5},{5,4},{6,7},{7,6},{8,9},{9,8},{10,11... | collective-permute-start | bytes 1327112 | tf_op jit(solution)/shard_map/ppermute | solution.py:445
  102.1 22.1 %collective-permute-start.14 = (bf16[4,144,768]{2,1,0:T(8,128)(2,1)S(1)}, bf16[4,144,768]{2,1,0:T(8,128)(2,1)}, u32[]{:S(2)}, u32[]{:S(2)}) collective-permute-start(bf16[4,144,768]{2,1,0:T(8,128)(2,1)S(1)} %pad_maximum_fusion.r_5_), channel_id=1, source_target_pairs={{0,1},{1,0},{2,3},{3,2},{4,5},{5,4},{6,7},{7,6},{8,9},{9,8},{10,11... | collective-permute-start | bytes 2654216 | tf_op jit(solution)/shard_map/ppermute | solution.py:445
  104.4 21.6 %collective-permute-start.16 = (bf16[4,144,768]{2,1,0:T(8,128)(2,1)S(1)}, bf16[4,144,768]{2,1,0:T(8,128)(2,1)}, u32[]{:S(2)}, u32[]{:S(2)}) collective-permute-start(bf16[4,144,768]{2,1,0:T(8,128)(2,1)S(1)} %collective-permute-done.11.r_7_), channel_id=1, source_target_pairs={{0,1},{1,0},{2,3},{3,2},{4,5},{5,4},{6,7},{7,6},{8,9},{9,8},{10,11... | collective-permute-start | bytes 2654216 | tf_op jit(solution)/shard_map/ppermute | solution.py:445
  121.1 4.9 %collective-permute-start.6 = (bf16[4,128,768]{2,1,0:T(8,128)(2,1)}, bf16[4,128,768]{2,1,0:T(8,128)(2,1)}, u32[]{:S(2)}, u32[]{:S(2)}) collective-permute-start(bf16[4,128,768]{2,1,0:T(8,128)(2,1)} %get-tuple-element.36), channel_id=1, source_target_pairs={{0,1},{1,0},{2,3},{3,2},{4,5},{5,4},{6,7},{7,6},{8,9},{9,8},{10,11... | collective-permute-start | bytes 2359304 | tf_op jit(solution)/shard_map/ppermute | solution.py:445
  121.9 4.0 %collective-permute-start.15 = (bf16[3,144,768]{2,1,0:T(8,128)(2,1)}, bf16[3,144,768]{2,1,0:T(8,128)(2,1)}, u32[]{:S(2)}, u32[]{:S(2)}) collective-permute-start(bf16[3,144,768]{2,1,0:T(8,128)(2,1)} %collective-permute-done.10.r_6_), channel_id=1, source_target_pairs={{0,1},{1,0},{2,3},{3,2},{4,5},{5,4},{6,7},{7,6},{8,9},{9,8},{10,11... | collective-permute-start | bytes 1990664 | tf_op jit(solution)/shard_map/ppermute | solution.py:445
  124.2 42.7 %collective-permute-start.19 = (bf16[16,144,384]{2,1,0:T(8,128)(2,1)S(1)}, bf16[16,144,384]{2,1,0:T(8,128)(2,1)}, u32[]{:S(2)}, u32[]{:S(2)}) collective-permute-start(bf16[16,144,384]{2,1,0:T(8,128)(2,1)S(1)} %constant_dynamic-slice_fusion.1), channel_id=1, source_target_pairs={{0,16},{16,0},{1,17},{17,1},{2,18},{18,2},{3,19},{19,3},{4,20},{20... | collective-permute-start | bytes 5308424 | tf_op jit(solution)/shard_map/ppermute | solution.py:451
  136.8 23.0 %collective-permute-start.18 = (bf16[2,512,768]{2,1,0:T(8,128)(2,1)}, bf16[2,512,768]{2,1,0:T(8,128)(2,1)}, u32[]{:S(2)}, u32[]{:S(2)}) collective-permute-start(bf16[2,512,768]{2,1,0:T(8,128)(2,1)} %get-tuple-element.42.r_2_), channel_id=1, source_target_pairs={{0,1},{1,2},{2,3},{3,4},{4,5},{5,6},{6,7},{7,8},{8,9},{9,10},{10,1... | collective-permute-start | bytes 4718600 | tf_op jit(solution)/shard_map/ppermute | solution.py:572
  166.9 3.9 %collective-permute-start.20 = (bf16[16,144,384]{2,1,0:T(8,128)(2,1)}, bf16[16,144,384]{2,1,0:T(8,128)(2,1)S(1)}, u32[]{:S(2)}, u32[]{:S(2)}) collective-permute-start(bf16[16,144,384]{2,1,0:T(8,128)(2,1)} %collective-permute-done.19.r_5_), channel_id=1, source_target_pairs={{0,1},{1,0},{2,3},{3,2},{4,5},{5,4},{6,7},{7,6},{8,9},{9,8},{10,11... | collective-permute-start | bytes 5308424 | tf_op jit(solution)/shard_map/ppermute | solution.py:445
  168.0 15.8 %collective-permute-start.22 = (bf16[16,48,384]{2,1,0:T(8,128)(2,1)S(1)}, bf16[16,48,384]{2,1,0:T(8,128)(2,1)S(1)}, u32[]{:S(2)}, u32[]{:S(2)}) collective-permute-start(bf16[16,48,384]{2,1,0:T(8,128)(2,1)S(1)} %constant_dynamic-slice_fusion), channel_id=1, source_target_pairs={{0,16},{16,0},{1,17},{17,1},{2,18},{18,2},{3,19},{19,3},{4,20},{20... | collective-permute-start | bytes 1769480 | tf_op jit(solution)/shard_map/ppermute | solution.py:451
  183.8 7.0 %collective-permute-start.23 = (bf16[16,48,384]{2,1,0:T(8,128)(2,1)S(1)}, bf16[16,48,384]{2,1,0:T(8,128)(2,1)S(1)}, u32[]{:S(2)}, u32[]{:S(2)}) collective-permute-start(bf16[16,48,384]{2,1,0:T(8,128)(2,1)S(1)} %collective-permute-done.22.r_8_), channel_id=1, source_target_pairs={{0,1},{1,0},{2,3},{3,2},{4,5},{5,4},{6,7},{7,6},{8,9},{9,8},{10,11... | collective-permute-start | bytes 1769480 | tf_op jit(solution)/shard_map/ppermute | solution.py:445
  183.8 7.0 %collective-permute-start.21 = (bf16[64,768]{1,0:T(8,128)(2,1)}, bf16[64,768]{1,0:T(8,128)(2,1)S(1)}, u32[]{:S(2)}, u32[]{:S(2)}) collective-permute-start(bf16[64,768]{1,0:T(8,128)(2,1)} %get-tuple-element.48), channel_id=1, source_target_pairs={{0,1},{1,2},{2,3},{3,4},{4,5},{5,6},{6,7},{7,8},{8,9},{9,10},{10,1... | collective-permute-start | bytes 294920 | tf_op jit(solution)/shard_map/ppermute | solution.py:604
  (20 other events, 275.1 us)
Sparse Core Ops, SparseCore 0:
  10.4 67.3 all-gather.2
